TPU v7x, 128 devices: a whole 4x4x4 slice. The times are simulated.
128 devices in a mesh: rows: 16 (over y, x), cols: 8 (over z, core).
Axes of the slice: x: 4, y: 4, z: 4, core: 2. Of those that a mesh axis runs over, the one named last changes fastest.
Arguments:
- affiliations: float32 [131072, 512], P(('rows', 'cols')), as said below
- tile_block: int32 [128, 240], P(('rows', 'cols')), may hold values from 0 to 1023, as said below
- tile_target: int32 [128, 240], P(('rows', 'cols')), may hold values from 0 to 7
- tile_pattern: int32 [128, 240], P(('rows', 'cols')), may hold values from 0 to 191
- tile_count: int32 [128], P(('rows', 'cols')), may hold values from 15 to 240, as said below
- block_home: int32 [1024], replicated, may hold values from 0 to 1023, as said below
- patterns: int32 [192, 5, 128], replicated, may hold values from 0 to 1073741823, as said below
Outputs:
- updated_affiliations: float32 [131072, 512], P(('rows', 'cols'))
Inputs may be any that keep to these rules, and one draw needn't show every extreme that they name: Live tiles of a device are the first tile_count of its slots, in order of their neighbour's owner row (storage block // 64); some device has exactly 240. `tile_block`: A live tile's neighbour is stored on a device of the same cols index and another rows index; a device's live tiles name at most 4 distinct blocks of one owner row, and in every draw some device names exactly 4 of every other owner row; a (target, neighbour) pair is live at most once on a device; slots past the count hold valid block numbers. `block_home`: A permutation of the node blocks. `patterns`: bits at rows 128 and beyond are zero. `affiliations`: Positive.
All inputs are finite; a program needn't handle non-finite values.
Results may differ from a plain program's by a relative error of at most 0.0003.
Values may be sent and summed in bfloat16 or wider, within the bound.
No kernel may reach another device: no remote copies, remote signals or barrier semaphores. Data moves between devices by JAX's collectives and lax.ppermute only.
A program may use at most 192 MiB of HBM per device.

v0:
```python
import functools

import jax
import jax.numpy as jnp
from jax import lax
from jax.experimental import pallas as pl
from jax.experimental.pallas import tpu as pltpu
from jax.sharding import Mesh
from jax.sharding import PartitionSpec as P

C = 512
BLOCK = 128
STEPS = 2
BPD = 8
SIDE = 4
CAP = 4
N_COLS = 8
NODES = 131072
UNIT = 1572864
PATTERNS = 192
TILES = 240
GROUP = 4
PARTS = 3
KEYS = PARTS * BPD
GROUPS = (TILES + KEYS * (GROUP - 1)) // GROUP + 2 * PARTS + 2
SLOTS = GROUPS * GROUP
EMPTY = PATTERNS * 64
FLOOR = 0.001
STEP_SIZE = 0.3 / NODES
OWN_ROWS = BPD * BLOCK
SENT_ROWS = OWN_ROWS + 16
PICKED = SIDE * CAP
HALF_ROWS = OWN_ROWS // 2

ALL = ("rows_0", "rows_1", "cols_0", "cols_1")
VMEM = pl.BlockSpec(memory_space=pltpu.VMEM)
SMEM = pl.BlockSpec(memory_space=pltpu.SMEM)


def pairs(first, second):
    out = []
    for y in range(SIDE):
        for x in range(SIDE):
            for z in range(4):
                for core in range(2):
                    dx, dy = (first, second) if core == 0 else (second, first)
                    sy, sx = (y + dy) % SIDE, (x + dx) % SIDE
                    out.append((((sy * 4 + sx) * 4 + z) * 2 + core, ((y * 4 + x) * 4 + z) * 2 + core))
    return out


def fetch(value, first, second):
    return lax.ppermute(value, ALL, pairs(first, second))


def sum_over_cols(part):
    for axis, size in (("cols_1", 2), ("cols_0", 4)):
        step = 1
        while step < size:
            part = part + lax.ppermute(part, axis, [(i, i ^ step) for i in range(size)])
            step *= 2
    return part


OWNERS = (
    ((1, 0), (1, 1), (1, 3), (3, 0), (3, 1), (3, 3), (0, 1), (0, 3), (0, 2)),
    ((2, 0), (2, 1), (2, 3), (2, 2)),
    ((1, 2), (3, 2)),
)


def clear(ref, size, value):
    def body(i, _):
        for j in range(8):
            ref[8 * i + j] = value
        return 0

    lax.fori_loop(0, size // 8, body, 0)


def ask_kernel(place, blocks, targets, count, home, requests, codes, rank, fill, base):
    first, second, core = place[0], place[1], place[2]
    clear(rank, 128, -1)
    clear(fill, 16, 0)
    clear(requests, 64, 0)
    base[0] = 0
    for part, owners in enumerate(OWNERS):
        for i, (m, k) in enumerate(owners):
            base[m * SIDE + k] = part * 512 + i * CAP

    def note(t, _):
        slot = home[blocks[t]]
        row = slot >> 6
        local = slot & (BPD - 1)
        y, x = row >> 2, row & (SIDE - 1)
        owner_first = jnp.where(core == 0, x, y)
        owner_second = jnp.where(core == 0, y, x)
        k = (owner_first - first) & (SIDE - 1)
        m = (owner_second - second) & (SIDE - 1)
        pair = m * SIDE + k
        seen = rank[pair * BPD + local]
        held = fill[pair]
        mine = jnp.minimum(jnp.where(seen < 0, held, seen), CAP - 1)
        rank[pair * BPD + local] = mine
        fill[pair] = jnp.where(seen < 0, held + 1, held)
        requests[pair * CAP + mine] = local
        codes[t] = base[pair] + mine + targets[t] * 64
        return 0

    lax.fori_loop(0, count[0], note, 0)


def ask(place, blocks, targets, count, home):
    i32 = jnp.int32
    return pl.pallas_call(
        ask_kernel,
        out_shape=(jax.ShapeDtypeStruct((64,), i32), jax.ShapeDtypeStruct((TILES,), i32)),
        in_specs=[SMEM] * 5,
        out_specs=(SMEM,) * 2,
        scratch_shapes=[pltpu.SMEM((128,), i32), pltpu.SMEM((16,), i32), pltpu.SMEM((16,), i32)],
        compiler_params=pltpu.CompilerParams(vmem_limit_bytes=2 << 20),
        name="ask",
    )(place, blocks, targets, count, home)


def sort_kernel(codes, pattern_ids, count, slots, group_target, part_start, per_key):
    clear(per_key, KEYS, 0)
    clear(slots, SLOTS, EMPTY)
    clear(group_target, GROUPS, 0)

    def tally(t, _):
        key = codes[t] >> 6
        per_key[key] = per_key[key] + 1
        return 0

    lax.fori_loop(0, count[0], tally, 0)
    group = jnp.int32(0)
    for part in range(PARTS):
        part_start[part] = group
        start = group
        for target in range(BPD):
            key = part * BPD + target
            size = (per_key[key] + GROUP - 1) >> 2
            per_key[key] = group * GROUP
            group = group + size
        group = start + jnp.maximum(2, (group - start + 1) & -2)
    part_start[PARTS] = group

    def put(t, _):
        code = codes[t]
        key = code >> 6
        at = per_key[key]
        per_key[key] = at + 1
        slots[at] = pattern_ids[t] * 64 + (code & 63)
        group_target[at >> 2] = key & (BPD - 1)
        return 0

    lax.fori_loop(0, count[0], put, 0)


def sort_tiles(codes, pattern_ids, count):
    i32 = jnp.int32
    return pl.pallas_call(
        sort_kernel,
        out_shape=(
            jax.ShapeDtypeStruct((SLOTS,), i32),
            jax.ShapeDtypeStruct((GROUPS,), i32),
            jax.ShapeDtypeStruct((PARTS + 1,), i32),
        ),
        in_specs=[SMEM] * 3,
        out_specs=(SMEM,) * 3,
        scratch_shapes=[pltpu.SMEM((KEYS,), i32)],
        compiler_params=pltpu.CompilerParams(vmem_limit_bytes=2 << 20),
        name="sort_tiles",
    )(codes, pattern_ids, count)


def sum_rows(total):
    high = total.astype(jnp.bfloat16).astype(jnp.float32)
    rest = total - high
    middle = rest.astype(jnp.bfloat16).astype(jnp.float32)
    low = rest - middle
    row = lax.broadcasted_iota(jnp.int32, (16, C), 0)
    out = jnp.where(row == 0, high, jnp.where(row == 1, middle, jnp.where(row == 2, low, 0.0)))
    return out.astype(jnp.bfloat16)


def first_kernel(current, sent):
    total = jnp.zeros((8, C), jnp.float32)
    for j in range(BPD):
        rows = current[pl.ds(j * BLOCK, BLOCK), :]
        sent[pl.ds(j * BLOCK, BLOCK), :] = rows.astype(jnp.bfloat16)
        total = total + jnp.sum(rows.reshape(BLOCK // 8, 8, C), axis=0)
    sent[pl.ds(OWN_ROWS, 16), :] = sum_rows(jnp.sum(total, axis=0, keepdims=True))


def first(current):
    return pl.pallas_call(
        first_kernel,
        out_shape=jax.ShapeDtypeStruct((SENT_ROWS, C), jnp.bfloat16),
        in_specs=[VMEM],
        out_specs=VMEM,
        compiler_params=pltpu.CompilerParams(vmem_limit_bytes=20 << 20),
        name="first",
    )(current)


def move(table, local, out, at):
    rows = pl.ds(pl.multiple_of(local * BLOCK, BLOCK), BLOCK)
    out[pl.ds(at * BLOCK, BLOCK), :] = table[rows, :]


def pick_early_kernel(asked, wanted, own, far1, far3, near, pass1, pass3, out1, out3):
    pass1[...] = far1[pl.ds(0, HALF_ROWS), :]
    pass3[...] = far3[pl.ds(HALF_ROWS, HALF_ROWS + 16), :]
    for m, out in ((1, out1), (3, out3)):
        for i, (k, table) in enumerate(((0, own), (1, far1), (3, far3))):
            for r in range(CAP):
                move(table, asked[m - 1, k * CAP + r], out, i * CAP + r)
    for r in range(CAP):
        move(far1, wanted[CAP + r], near, r)
        move(far3, wanted[3 * CAP + r], near, CAP + r)


def pick_early(asked, wanted, own, far1, far3):
    b16 = jnp.bfloat16
    out = jax.ShapeDtypeStruct((3 * CAP * BLOCK, C), b16)
    return pl.pallas_call(
        pick_early_kernel,
        out_shape=(
            jax.ShapeDtypeStruct((2 * CAP * BLOCK, C), b16),
            jax.ShapeDtypeStruct((HALF_ROWS, C), b16),
            jax.ShapeDtypeStruct((HALF_ROWS + 16, C), b16),
            out,
            out,
        ),
        in_specs=[SMEM] * 2 + [VMEM] * 3,
        out_specs=(VMEM,) * 5,
        compiler_params=pltpu.CompilerParams(vmem_limit_bytes=20 << 20),
        name="pick_early",
    )(asked, wanted, own, far1, far3)


def pick_late_kernel(asked, wanted, own, far1, far3, low2, high2, near, out1, out3, out2, line, far2):
    far2[pl.ds(0, HALF_ROWS), :] = low2[...]
    far2[pl.ds(HALF_ROWS, HALF_ROWS + 16), :] = high2[...]
    tables = ((0, own), (1, far1), (3, far3), (2, far2))
    for r in range(CAP):
        move(far2, asked[0, 2 * CAP + r], out1, r)
        move(far2, asked[2, 2 * CAP + r], out3, r)
        move(far2, wanted[2 * CAP + r], near, r)
    for i, (k, table) in enumerate(tables):
        for r in range(CAP):
            move(table, asked[1, k * CAP + r], out2, i * CAP + r)
    rows = sum(t[pl.ds(OWN_ROWS, 16), :].astype(jnp.float32) for _, t in tables)
    sums = jnp.sum(rows, axis=0, keepdims=True)
    line[...] = jnp.broadcast_to(sums, (8, C))


def pick_late(asked, wanted, own, far1, far3, low2, high2):
    b16 = jnp.bfloat16
    piece = jax.ShapeDtypeStruct((CAP * BLOCK, C), b16)
    return pl.pallas_call(
        pick_late_kernel,
        out_shape=(
            piece,
            piece,
            piece,
            jax.ShapeDtypeStruct((PICKED * BLOCK, C), b16),
            jax.ShapeDtypeStruct((8, C), jnp.float32),
        ),
        in_specs=[SMEM] * 2 + [VMEM] * 5,
        out_specs=(VMEM,) * 5,
        scratch_shapes=[pltpu.VMEM((SENT_ROWS, C), b16)],
        compiler_params=pltpu.CompilerParams(vmem_limit_bytes=20 << 20),
        name="pick_late",
    )(asked, wanted, own, far1, far3, low2, high2)


def tile_kernel(part, table_count, resume, finish, *refs):
    refs = list(refs)
    slots, group_target, part_start, words, own = refs[:5]
    tables = refs[5 : 5 + table_count]
    refs = refs[5 + table_count :]
    if resume:
        earlier = refs.pop(0)
    if finish:
        current, all_sums, fresh = refs[:3]
        refs = refs[3:]
        if finish == "more":
            sent = refs.pop(0)
    total, score_a, score_b, bits = refs[:4]

    row = lax.broadcasted_iota(jnp.int32, (BLOCK, BLOCK), 0)
    bits[...] = lax.shift_left(jnp.ones_like(row), lax.rem(row, 30))
    total[...] = earlier[...] if resume else jnp.zeros_like(total)
    sub = lax.broadcasted_iota(jnp.int32, (8, BLOCK), 0)
    if table_count == 1:
        held = tables[0]
    else:
        held = refs[4]
        at = 0
        for table in tables:
            held[pl.ds(at, table.shape[0]), :] = table[...]
            at += table.shape[0]

    def rows_of(index):
        return pl.ds(pl.multiple_of(index * BLOCK, BLOCK), BLOCK)

    def word_rows(pattern):
        rows = []
        for v in range(BLOCK // 8):
            low, high = 8 * v // 30, (8 * v + 7) // 30
            chunk = jnp.broadcast_to(words[pattern, low : low + 1, :], (8, BLOCK))
            if high != low:
                other = jnp.broadcast_to(words[pattern, high : high + 1, :], (8, BLOCK))
                chunk = jnp.where(sub + 8 * v < 30 * high, chunk, other)
            rows.append(chunk)
        return jnp.concatenate(rows, axis=0)

    def remote(group, i):
        return held[rows_of(slots[group * GROUP + i] & 63), :]

    def score(group, out):
        mine = own[rows_of(group_target[group]), :]
        for i in range(GROUP):
            out[:, i * BLOCK : (i + 1) * BLOCK] = lax.dot_general(
                mine,
                remote(group, i),
                (((1,), (1,)), ((), ())),
                preferred_element_type=jnp.float32,
            )

    def add(group, scores):
        weights = []
        for i in range(GROUP):
            packed = word_rows(slots[group * GROUP + i] >> 6)
            negative = jnp.minimum(scores[:, i * BLOCK : (i + 1) * BLOCK] * (-1.0 / UNIT), -FLOOR)
            weight = 1.0 / (1.0 - jnp.exp(negative))
            linked = (packed & bits[...]) != 0
            weights.append(jnp.where(linked, weight, 0.0).astype(jnp.bfloat16))
        total[rows_of(group_target[group]), :] += jnp.dot(
            jnp.concatenate(weights, axis=1),
            jnp.concatenate([remote(group, i) for i in range(GROUP)], axis=0),
            preferred_element_type=jnp.float32,
        )

    start, stop = part_start[part], part_start[part + 1]
    score(start, score_a)

    def two(i, _):
        group = start + 2 * i
        score(group + 1, score_b)
        add(group, score_a)
        score(jnp.minimum(group + 2, stop - 1), score_a)
        add(group + 1, score_b)
        return 0

    lax.fori_loop(0, (stop - start) >> 1, two, 0)

    if finish:
        col_sums = all_sums[0:1, :]
        moved_sums = jnp.zeros((8, C), jnp.float32)
        for j in range(BPD):
            at = pl.ds(j * BLOCK, BLOCK)
            moved = jnp.maximum(current[at, :] + STEP_SIZE * (total[at, :] - col_sums), 0.0)
            fresh[at, :] = moved
            if finish == "more":
                sent[at, :] = moved.astype(jnp.bfloat16)
                moved_sums = moved_sums + jnp.sum(moved.reshape(BLOCK // 8, 8, C), axis=0)
        if finish == "more":
            sent[pl.ds(OWN_ROWS, 16), :] = sum_rows(jnp.sum(moved_sums, axis=0, keepdims=True))


def run_tiles(name, part, lists, words, own, tables, earlier=None, current=None, sums=None, finish=""):
    f32 = jnp.float32
    blocks = jax.ShapeDtypeStruct((OWN_ROWS, C), f32)
    args = [*lists, words, own, *tables]
    specs = [SMEM] * 3 + [VMEM] * (2 + len(tables))
    scratch = []
    out = [blocks]
    if earlier is not None:
        args.append(earlier)
        specs.append(VMEM)
    if finish:
        args += [current, sums]
        specs += [VMEM] * 2
        scratch.append(pltpu.VMEM((OWN_ROWS, C), f32))
        if finish == "more":
            out.append(jax.ShapeDtypeStruct((SENT_ROWS, C), jnp.bfloat16))
    scratch += [
        pltpu.VMEM((BLOCK, GROUP * BLOCK), f32),
        pltpu.VMEM((BLOCK, GROUP * BLOCK), f32),
        pltpu.VMEM((BLOCK, BLOCK), jnp.int32),
    ]
    if len(tables) > 1:
        scratch.append(pltpu.VMEM((sum(t.shape[0] for t in tables), C), jnp.bfloat16))
    return pl.pallas_call(
        functools.partial(tile_kernel, part, len(tables), earlier is not None, finish),
        out_shape=tuple(out),
        in_specs=specs,
        out_specs=(VMEM,) * len(out),
        scratch_shapes=scratch,
        compiler_params=pltpu.CompilerParams(vmem_limit_bytes=24 << 20),
        name=name,
    )(*args)


def per_device(affiliations, tile_block, tile_target, tile_pattern, tile_count, block_home, patterns):
    y, x = lax.axis_index("rows_0"), lax.axis_index("rows_1")
    core = lax.axis_index("cols_1")
    place = jnp.stack([jnp.where(core == 0, x, y), jnp.where(core == 0, y, x), core])
    current = affiliations
    own = first(current)
    requests, codes = ask(
        place.astype(jnp.int32), tile_block[0], tile_target[0], tile_count, block_home
    )
    requests = requests.reshape(SIDE, PICKED)
    asked = jnp.stack([fetch(requests[m], 0, SIDE - m) for m in (1, 2, 3)])
    words = jnp.concatenate([patterns, jnp.zeros((1, *patterns.shape[1:]), jnp.int32)], axis=0)

    lists = sort_tiles(codes, tile_pattern[0], tile_count)
    for step in range(STEPS):
        far1, far3 = fetch(own, 1, 0), fetch(own, 3, 0)
        near1, pass1, pass3, out1, out3 = pick_early(asked, requests[0], own, far1, far3)
        low2, high2 = fetch(pass1, 1, 0), fetch(pass3, 3, 0)
        side1, side3 = fetch(out1, 0, 1), fetch(out3, 0, 3)
        lists, low2, high2 = lax.optimization_barrier((lists, low2, high2))
        near2, out1, out3, out2, line = pick_late(asked, requests[0], own, far1, far3, low2, high2)
        lines = tuple(fetch(line, 0, m) for m in (1, 3, 2))
        lines, out2, side1, side3 = lax.optimization_barrier((lines, out2, side1, side3))
        side2 = fetch(out2, 0, 2)
        late1, late3 = fetch(out1, 0, 1), fetch(out3, 0, 3)
        col_sums = sum_over_cols(line + lines[0] + lines[1] + lines[2])
        tables = (side1, side3, near1, near2)
        (total,) = run_tiles("sides", 0, lists, words, own, tables)
        (total,) = run_tiles("across", 1, lists, words, own, (side2,), total)
        total, late1, late3 = lax.optimization_barrier((total, late1, late3))
        finish = "more" if step < STEPS - 1 else "end"
        current, *own_next = run_tiles(
            "late", 2, lists, words, own, (late1, late3), total, current, col_sums, finish
        )
        if own_next:
            (own,) = own_next
    return current


def solution(mesh):
    torus = Mesh(mesh.devices.reshape(4, 4, 4, 2), ALL)
    return jax.shard_map(
        per_device,
        mesh=torus,
        in_specs=(P(ALL, None), P(ALL, None), P(ALL, None), P(ALL, None), P(ALL), P(), P()),
        out_specs=P(ALL, None),
        check_vma=False,
    )
```

profile of v0, /device:TPU:32, one launch (start us, length us, event | category | flops | bytes accessed | tf_op | source)
XLA Modules:
  0.0 168.2 jit_solution(10105784684886965626)
XLA Ops:
  0.0 1.6 copy-done
  1.6 0.1 first.1.own.refs_4_
  1.7 1.6 collective-permute-start.4
  3.3 1.7 %collective-permute-start.3 = (bf16[1040,512]{1,0:T(8,128)(2,1)S(1)}, bf16[1040,512]{1,0:T(8,128)(2,1)S(1)}, u32[]{:S(2)}, u32[]{:S(2)}) collective-permute-start(bf16[1040,512]{1,0:T(8,128)(2,1)S(1)} %first.1.own.refs_4_), channel_id=1, source_target_pairs={{8,0},{33,1},{10,2},{35,3},{12,4},{37,5},{14,6},{39,7},{16,8},{41,... | collective-permute-start | bytes 3194888 | tf_op jit(solution)/shard_map/ppermute | solution.py:53
  5.8 3.9 %ask.1 = (s32[64]{0:T(128)S(1)}, s32[240]{0:T(256)S(1)}) custom-call(s32[3]{0:T(128)S(1)} %pad_add_fusion.1.place, s32[240]{0:T(256)S(1)} %bitcast.9, s32[240]{0:T(256)S(1)} %bitcast.10, s32[1]{0:T(128)S(6)} %copy.9.count, s32[1024]{0:T(1024)S(1)} %copy-done.2), custom_call_target="tpu_custom_call" | custom-call | tf_op jit(solution)/shard_map/ask/pallas_call | solution.py:115
  9.7 2.1 %collective-permute-start.2 = (s32[16]{0:T(128)S(1)}, s32[16]{0:T(128)S(1)}, u32[]{:S(2)}, u32[]{:S(2)}) collective-permute-start(s32[16]{0:T(128)S(1)} %get-tuple-element.116), channel_id=1, source_target_pairs={{32,0},{9,1},{34,2},{11,3},{36,4},{13,5},{38,6},{15,7},{40,8},{17,... | collective-permute-start | bytes 200 | tf_op jit(solution)/shard_map/ppermute | solution.py:53
  11.9 0.9 collective-permute-start.1
  12.8 1.2 collective-permute-start
  14.0 3.0 %collective-permute-done.1 = s32[16]{0:T(128)S(1)} collective-permute-done((s32[16]{0:T(128)S(1)}, s32[16]{0:T(128)S(1)}, u32[]{:S(2)}, u32[]{:S(2)}) %collective-permute-start.1) | collective-permute-done | bytes 96 | tf_op jit(solution)/shard_map/ppermute | solution.py:53
  17.0 0.6 collective-permute-done
  17.6 0.4 collective-permute-done.4.far3
  18.0 0.3 collective-permute-done.3.far1
  18.3 0.9 pick_early.2
  19.2 3.1 %collective-permute-start.10 = (bf16[1536,512]{1,0:T(8,128)(2,1)S(1)}, bf16[1536,512]{1,0:T(8,128)(2,1)S(1)}, u32[]{:S(2)}, u32[]{:S(2)}) collective-permute-start(bf16[1536,512]{1,0:T(8,128)(2,1)S(1)} %get-tuple-element.74), channel_id=1, source_target_pairs={{32,0},{9,1},{34,2},{11,3},{36,4},{13,5},{38,6},{15,7},{40,8},{17,... | collective-permute-start | bytes 4718600 | tf_op jit(solution)/shard_map/ppermute | solution.py:53
  22.3 1.5 collective-permute-start.6
  23.8 1.7 %collective-permute-start.5 = (bf16[512,512]{1,0:T(8,128)(2,1)S(1)}, bf16[512,512]{1,0:T(8,128)(2,1)S(1)}, u32[]{:S(2)}, u32[]{:S(2)}) collective-permute-start(bf16[512,512]{1,0:T(8,128)(2,1)S(1)} %get-tuple-element.65), channel_id=1, source_target_pairs={{8,0},{33,1},{10,2},{35,3},{12,4},{37,5},{14,6},{39,7},{16,8},{41,... | collective-permute-start | bytes 1572872 | tf_op jit(solution)/shard_map/ppermute | solution.py:53
  25.5 3.7 %sort_tiles.1 = (s32[344]{0:T(512)S(1)}, s32[86]{0:T(128)S(1)}, s32[4]{0:T(128)S(1)}) custom-call(s32[240]{0:T(256)S(1)} %get-tuple-element.60.codes, s32[240]{0:T(256)S(1)} %bitcast.11, s32[1]{0:T(128)S(6)} %copy.9.count), custom_call_target="tpu_custom_call" | custom-call | tf_op jit(solution)/shard_map/sort_tiles/pallas_call | solution.py:163
  29.2 9.4 %collective-permute-done.5.low2 = bf16[512,512]{1,0:T(8,128)(2,1)S(1)} collective-permute-done((bf16[512,512]{1,0:T(8,128)(2,1)S(1)}, bf16[512,512]{1,0:T(8,128)(2,1)S(1)}, u32[]{:S(2)}, u32[]{:S(2)}) %collective-permute-start.5) | collective-permute-done | bytes 524320 | tf_op jit(solution)/shard_map/ppermute | solution.py:53
  38.7 0.9 pick_late.2
  39.6 2.3 %collective-permute-start.9 = (f32[8,512]{1,0:T(8,128)S(1)}, f32[8,512]{1,0:T(8,128)S(1)}, u32[]{:S(2)}, u32[]{:S(2)}) collective-permute-start(f32[8,512]{1,0:T(8,128)S(1)} %get-tuple-element.72), channel_id=1, source_target_pairs={{64,0},{17,1},{66,2},{19,3},{68,4},{21,5},{70,6},{23,7},{72,8},{25... | collective-permute-start | bytes 49160 | tf_op jit(solution)/shard_map/ppermute | solution.py:53
  41.9 1.9 %collective-permute-start.8 = (f32[8,512]{1,0:T(8,128)S(1)}, f32[8,512]{1,0:T(8,128)S(1)}, u32[]{:S(2)}, u32[]{:S(2)}) collective-permute-start(f32[8,512]{1,0:T(8,128)S(1)} %get-tuple-element.72), channel_id=1, source_target_pairs={{96,0},{25,1},{98,2},{27,3},{100,4},{29,5},{102,6},{31,7},{104,8},... | collective-permute-start | bytes 49160 | tf_op jit(solution)/shard_map/ppermute | solution.py:53
  43.8 1.3 collective-permute-start.7
  45.1 3.3 %collective-permute-done.9 = f32[8,512]{1,0:T(8,128)S(1)} collective-permute-done((f32[8,512]{1,0:T(8,128)S(1)}, f32[8,512]{1,0:T(8,128)S(1)}, u32[]{:S(2)}, u32[]{:S(2)}) %collective-permute-start.9) | collective-permute-done | bytes 16416 | tf_op jit(solution)/shard_map/ppermute | solution.py:53
  48.4 0.7 collective-permute-start.12
  49.1 1.7 %collective-permute-start.13 = (bf16[512,512]{1,0:T(8,128)(2,1)S(1)}, bf16[512,512]{1,0:T(8,128)(2,1)S(1)}, u32[]{:S(2)}, u32[]{:S(2)}) collective-permute-start(bf16[512,512]{1,0:T(8,128)(2,1)S(1)} %get-tuple-element.81), channel_id=1, source_target_pairs={{32,0},{9,1},{34,2},{11,3},{36,4},{13,5},{38,6},{15,7},{40,8},{17,... | collective-permute-start | bytes 1572872 | tf_op jit(solution)/shard_map/ppermute | solution.py:53
  50.8 0.3 collective-permute-start.14
  51.2 1.2 collective-permute-done.15
  52.5 3.6 %collective-permute-done.16 = f32[8,512]{1,0:T(8,128)S(1)} collective-permute-done((f32[8,512]{1,0:T(8,128)S(1)}, f32[8,512]{1,0:T(8,128)S(1)}, u32[]{:S(2)}, u32[]{:S(2)}) %collective-permute-start.16) | collective-permute-done | bytes 16416 | tf_op jit(solution)/shard_map/ppermute | solution.py:60
  56.1 3.0 %collective-permute-start.17 = (f32[8,512]{1,0:T(8,128)S(1)}, f32[8,512]{1,0:T(8,128)S(1)}, u32[]{:S(2)}, u32[]{:S(2)}) collective-permute-start(f32[8,512]{1,0:T(8,128)S(1)} %add.42), channel_id=1, source_target_pairs={{0,4},{2,6},{4,0},{6,2},{1,5},{3,7},{5,1},{7,3},{8,12},{10,14},{12... | collective-permute-start | bytes 49160 | tf_op jit(solution)/shard_map/ppermute | solution.py:60
  59.1 0.3 copy.8
  59.5 7.2 %sides.2.refs_6_ = f32[1024,512]{1,0:T(8,128)S(1)} custom-call(s32[344]{0:T(512)S(1)} %get-tuple-element.92.refs_0_, s32[86]{0:T(128)S(1)} %get-tuple-element.93.refs_1_, s32[4]{0:T(128)S(1)} %get-tuple-element.94.refs_2_, s32[193,5,128]{2,1,0:T(8,128)S(1)} %concatenate.3.refs_3_, bf16[1040,512]{1,0:T(8,128)(2,1)S(1)} %first.1.own.refs_4_, ...), custom_call_target="tpu_custom_call" | custom-call | tf_op jit(solution)/shard_map/sides/pallas_call | solution.py:398
  66.7 9.4 %collective-permute-done.12.refs_5_ = bf16[2048,512]{1,0:T(8,128)(2,1)S(1)} collective-permute-done((bf16[2048,512]{1,0:T(8,128)(2,1)S(1)}, bf16[2048,512]{1,0:T(8,128)(2,1)S(1)}, u32[]{:S(2)}, u32[]{:S(2)}) %collective-permute-start.12) | collective-permute-done | bytes 2097184 | tf_op jit(solution)/shard_map/ppermute | solution.py:53
  76.1 4.2 %across.2.refs_7_ = f32[1024,512]{1,0:T(8,128)S(1)} custom-call(s32[344]{0:T(512)S(1)} %get-tuple-element.92.refs_0_, s32[86]{0:T(128)S(1)} %get-tuple-element.93.refs_1_, s32[4]{0:T(128)S(1)} %get-tuple-element.94.refs_2_, s32[193,5,128]{2,1,0:T(8,128)S(1)} %concatenate.3.refs_3_, bf16[1040,512]{1,0:T(8,128)(2,1)S(1)} %first.1.own.refs_4_, ...), custom_call_target="tpu_custom_call" | custom-call | tf_op jit(solution)/shard_map/across/pallas_call | solution.py:398
  80.3 0.3 collective-permute-done.13.refs_5_
  80.6 1.0 collective-permute-done.14.refs_6_
  81.7 3.9 %late.2 = (f32[1024,512]{1,0:T(8,128)S(1)}, bf16[1040,512]{1,0:T(8,128)(2,1)S(1)}) custom-call(s32[344]{0:T(512)S(1)} %get-tuple-element.92.refs_0_, s32[86]{0:T(128)S(1)} %get-tuple-element.93.refs_1_, s32[4]{0:T(128)S(1)} %get-tuple-element.94.refs_2_, s32[193,5,128]{2,1,0:T(8,128)S(1)} %concatenate.3.refs_3_, bf16[1040,512]{1,0:T(8,128)(2,1)S(1)} %first.1.own.refs_4_, ...), custom_call_target="tpu_custom_call" | custom-call | tf_op jit(solution)/shard_map/late/pallas_call | solution.py:398
  85.6 0.3 collective-permute-start.19
  85.9 3.0 %collective-permute-start.18 = (bf16[1040,512]{1,0:T(8,128)(2,1)S(1)}, bf16[1040,512]{1,0:T(8,128)(2,1)S(1)}, u32[]{:S(2)}, u32[]{:S(2)}) collective-permute-start(bf16[1040,512]{1,0:T(8,128)(2,1)S(1)} %get-tuple-element.89.own.refs_4_), channel_id=1, source_target_pairs={{8,0},{33,1},{10,2},{35,3},{12,4},{37,5},{14,6},{39,7},{16,8},{41,... | collective-permute-start | bytes 3194888 | tf_op jit(solution)/shard_map/ppermute | solution.py:53
  88.9 12.9 %collective-permute-done.19.far3 = bf16[1040,512]{1,0:T(8,128)(2,1)S(1)} collective-permute-done((bf16[1040,512]{1,0:T(8,128)(2,1)S(1)}, bf16[1040,512]{1,0:T(8,128)(2,1)S(1)}, u32[]{:S(2)}, u32[]{:S(2)}) %collective-permute-start.19) | collective-permute-done | bytes 1064992 | tf_op jit(solution)/shard_map/ppermute | solution.py:53
  101.9 0.9 pick_early.3
  102.8 1.7 collective-permute-start.25
  104.4 0.4 collective-permute-start.26
  104.9 1.4 collective-permute-start.21
  106.2 1.9 %collective-permute-start.20 = (bf16[512,512]{1,0:T(8,128)(2,1)S(1)}, bf16[512,512]{1,0:T(8,128)(2,1)S(1)}, u32[]{:S(2)}, u32[]{:S(2)}) collective-permute-start(bf16[512,512]{1,0:T(8,128)(2,1)S(1)} %get-tuple-element.90), channel_id=1, source_target_pairs={{8,0},{33,1},{10,2},{35,3},{12,4},{37,5},{14,6},{39,7},{16,8},{41,... | collective-permute-start | bytes 1572872 | tf_op jit(solution)/shard_map/ppermute | solution.py:53
  108.2 13.0 %collective-permute-done.20.low2 = bf16[512,512]{1,0:T(8,128)(2,1)S(1)} collective-permute-done((bf16[512,512]{1,0:T(8,128)(2,1)S(1)}, bf16[512,512]{1,0:T(8,128)(2,1)S(1)}, u32[]{:S(2)}, u32[]{:S(2)}) %collective-permute-start.20) | collective-permute-done | bytes 524320 | tf_op jit(solution)/shard_map/ppermute | solution.py:53
  121.2 0.2 collective-permute-done.21.high2
  121.3 0.9 pick_late.3
  122.2 1.4 collective-permute-start.24
  123.6 2.5 %collective-permute-start.23 = (f32[8,512]{1,0:T(8,128)S(1)}, f32[8,512]{1,0:T(8,128)S(1)}, u32[]{:S(2)}, u32[]{:S(2)}) collective-permute-start(f32[8,512]{1,0:T(8,128)S(1)} %get-tuple-element.97), channel_id=1, source_target_pairs={{96,0},{25,1},{98,2},{27,3},{100,4},{29,5},{102,6},{31,7},{104,8},... | collective-permute-start | bytes 49160 | tf_op jit(solution)/shard_map/ppermute | solution.py:53
  126.1 0.7 collective-permute-start.22
  126.8 2.7 %collective-permute-done.24 = f32[8,512]{1,0:T(8,128)S(1)} collective-permute-done((f32[8,512]{1,0:T(8,128)S(1)}, f32[8,512]{1,0:T(8,128)S(1)}, u32[]{:S(2)}, u32[]{:S(2)}) %collective-permute-start.24) | collective-permute-done | bytes 16416 | tf_op jit(solution)/shard_map/ppermute | solution.py:53
  129.5 0.4 collective-permute-done.22
  129.9 0.7 collective-permute-start.27
  130.6 2.1 %collective-permute-start.28 = (bf16[512,512]{1,0:T(8,128)(2,1)S(1)}, bf16[512,512]{1,0:T(8,128)(2,1)S(1)}, u32[]{:S(2)}, u32[]{:S(2)}) collective-permute-start(bf16[512,512]{1,0:T(8,128)(2,1)S(1)} %get-tuple-element.106), channel_id=1, source_target_pairs={{32,0},{9,1},{34,2},{11,3},{36,4},{13,5},{38,6},{15,7},{40,8},{17,... | collective-permute-start | bytes 1572872 | tf_op jit(solution)/shard_map/ppermute | solution.py:53
  132.8 1.2 collective-permute-done.30
  133.9 1.2 collective-permute-start.31
  135.2 2.5 %collective-permute-done.31 = f32[8,512]{1,0:T(8,128)S(1)} collective-permute-done((f32[8,512]{1,0:T(8,128)S(1)}, f32[8,512]{1,0:T(8,128)S(1)}, u32[]{:S(2)}, u32[]{:S(2)}) %collective-permute-start.31) | collective-permute-done | bytes 16416 | tf_op jit(solution)/shard_map/ppermute | solution.py:60
  137.7 4.1 %collective-permute-start.32 = (f32[8,512]{1,0:T(8,128)S(1)}, f32[8,512]{1,0:T(8,128)S(1)}, u32[]{:S(2)}, u32[]{:S(2)}) collective-permute-start(f32[8,512]{1,0:T(8,128)S(1)} %add.48), channel_id=1, source_target_pairs={{0,4},{2,6},{4,0},{6,2},{1,5},{3,7},{5,1},{7,3},{8,12},{10,14},{12... | collective-permute-start | bytes 49160 | tf_op jit(solution)/shard_map/ppermute | solution.py:60
  141.8 7.3 %sides.3.refs_6_ = f32[1024,512]{1,0:T(8,128)S(1)} custom-call(s32[344]{0:T(512)S(1)} %get-tuple-element.92.refs_0_, s32[86]{0:T(128)S(1)} %get-tuple-element.93.refs_1_, s32[4]{0:T(128)S(1)} %get-tuple-element.94.refs_2_, s32[193,5,128]{2,1,0:T(8,128)S(1)} %concatenate.3.refs_3_, bf16[1040,512]{1,0:T(8,128)(2,1)S(1)} %get-tuple-element.89.own.refs_4_, ...), custom_call_target="tpu_custom_call" | custom-call | tf_op jit(solution)/shard_map/sides/pallas_call | solution.py:398
  149.1 8.4 %collective-permute-done.27.refs_5_ = bf16[2048,512]{1,0:T(8,128)(2,1)S(1)} collective-permute-done((bf16[2048,512]{1,0:T(8,128)(2,1)S(1)}, bf16[2048,512]{1,0:T(8,128)(2,1)S(1)}, u32[]{:S(2)}, u32[]{:S(2)}) %collective-permute-start.27) | collective-permute-done | bytes 2097184 | tf_op jit(solution)/shard_map/ppermute | solution.py:53
  157.5 4.2 %across.3.refs_7_ = f32[1024,512]{1,0:T(8,128)S(1)} custom-call(s32[344]{0:T(512)S(1)} %get-tuple-element.92.refs_0_, s32[86]{0:T(128)S(1)} %get-tuple-element.93.refs_1_, s32[4]{0:T(128)S(1)} %get-tuple-element.94.refs_2_, s32[193,5,128]{2,1,0:T(8,128)S(1)} %concatenate.3.refs_3_, bf16[1040,512]{1,0:T(8,128)(2,1)S(1)} %get-tuple-element.89.own.refs_4_, ...), custom_call_target="tpu_custom_call" | custom-call | tf_op jit(solution)/shard_map/across/pallas_call | solution.py:398
  161.8 0.6 collective-permute-done.28.refs_5_
  162.3 0.7 collective-permute-done.29.refs_6_
  163.1 5.1 %late.3 = f32[1024,512]{1,0:T(8,128)} custom-call(s32[344]{0:T(512)S(1)} %get-tuple-element.92.refs_0_, s32[86]{0:T(128)S(1)} %get-tuple-element.93.refs_1_, s32[4]{0:T(128)S(1)} %get-tuple-element.94.refs_2_, s32[193,5,128]{2,1,0:T(8,128)S(1)} %concatenate.3.refs_3_, bf16[1040,512]{1,0:T(8,128)(2,1)S(1)} %get-tuple-element.89.own.refs_4_, ...), custom_call_target="tpu_custom_call" | custom-call | tf_op jit(solution)/shard_map/late/pallas_call | solution.py:398
  (42 shorter events, 0.6 us)
Async XLA Ops:
  0.0 1.6 copy-start
  1.6 4.2 %copy-start.2 = (s32[1024]{0:T(1024)S(1)}, s32[1024]{0:T(1024)}, u32[]{:S(2)}) copy-start(s32[1024]{0:T(1024)} %home.1) | copy-start | bytes 12292
  1.6 4.2 %copy-start.3 = (s32[1,240]{1,0:T(1,128)S(1)}, s32[1,240]{1,0:T(1,128)}, u32[]{:S(2)}) copy-start(s32[1,240]{1,0:T(1,128)} %param.8) | copy-start | bytes 2884
  1.6 4.2 %copy-start.4 = (s32[1,240]{1,0:T(1,128)S(1)}, s32[1,240]{1,0:T(1,128)}, u32[]{:S(2)}) copy-start(s32[1,240]{1,0:T(1,128)} %param.9) | copy-start | bytes 2884
  1.7 16.3 %collective-permute-start.4 = (bf16[1040,512]{1,0:T(8,128)(2,1)S(1)}, bf16[1040,512]{1,0:T(8,128)(2,1)S(1)}, u32[]{:S(2)}, u32[]{:S(2)}) collective-permute-start(bf16[1040,512]{1,0:T(8,128)(2,1)S(1)} %first.1.own.refs_4_), channel_id=1, source_target_pairs={{24,0},{97,1},{26,2},{99,3},{28,4},{101,5},{30,6},{103,7},{0,8},{1... | collective-permute-start | bytes 3194888 | tf_op jit(solution)/shard_map/ppermute | solution.py:53
  3.3 15.0 %collective-permute-start.3 = (bf16[1040,512]{1,0:T(8,128)(2,1)S(1)}, bf16[1040,512]{1,0:T(8,128)(2,1)S(1)}, u32[]{:S(2)}, u32[]{:S(2)}) collective-permute-start(bf16[1040,512]{1,0:T(8,128)(2,1)S(1)} %first.1.own.refs_4_), channel_id=1, source_target_pairs={{8,0},{33,1},{10,2},{35,3},{12,4},{37,5},{14,6},{39,7},{16,8},{41,... | collective-permute-start | bytes 3194888 | tf_op jit(solution)/shard_map/ppermute | solution.py:53
  9.7 4.2 %collective-permute-start.2 = (s32[16]{0:T(128)S(1)}, s32[16]{0:T(128)S(1)}, u32[]{:S(2)}, u32[]{:S(2)}) collective-permute-start(s32[16]{0:T(128)S(1)} %get-tuple-element.116), channel_id=1, source_target_pairs={{32,0},{9,1},{34,2},{11,3},{36,4},{13,5},{38,6},{15,7},{40,8},{17,... | collective-permute-start | bytes 200 | tf_op jit(solution)/shard_map/ppermute | solution.py:53
  11.9 5.1 %collective-permute-start.1 = (s32[16]{0:T(128)S(1)}, s32[16]{0:T(128)S(1)}, u32[]{:S(2)}, u32[]{:S(2)}) collective-permute-start(s32[16]{0:T(128)S(1)} %get-tuple-element.117), channel_id=1, source_target_pairs={{64,0},{17,1},{66,2},{19,3},{68,4},{21,5},{70,6},{23,7},{72,8},{25... | collective-permute-start | bytes 200 | tf_op jit(solution)/shard_map/ppermute | solution.py:53
  12.8 4.8 %collective-permute-start = (s32[16]{0:T(128)S(1)}, s32[16]{0:T(128)S(1)}, u32[]{:S(2)}, u32[]{:S(2)}) collective-permute-start(s32[16]{0:T(128)S(1)} %get-tuple-element.118), channel_id=1, source_target_pairs={{96,0},{25,1},{98,2},{27,3},{100,4},{29,5},{102,6},{31,7},{104,8},... | collective-permute-start | bytes 200 | tf_op jit(solution)/shard_map/ppermute | solution.py:53
  18.3 7.2 %copy-start.5 = (s32[1,240]{1,0:T(1,128)S(1)}, s32[1,240]{1,0:T(1,128)}, u32[]{:S(2)}) copy-start(s32[1,240]{1,0:T(1,128)} %param.10) | copy-start | bytes 2884
  19.2 29.2 %collective-permute-start.10 = (bf16[1536,512]{1,0:T(8,128)(2,1)S(1)}, bf16[1536,512]{1,0:T(8,128)(2,1)S(1)}, u32[]{:S(2)}, u32[]{:S(2)}) collective-permute-start(bf16[1536,512]{1,0:T(8,128)(2,1)S(1)} %get-tuple-element.74), channel_id=1, source_target_pairs={{32,0},{9,1},{34,2},{11,3},{36,4},{13,5},{38,6},{15,7},{40,8},{17,... | collective-permute-start | bytes 4718600 | tf_op jit(solution)/shard_map/ppermute | solution.py:53
  22.3 26.1 %collective-permute-start.11 = (bf16[1536,512]{1,0:T(8,128)(2,1)S(1)}, bf16[1536,512]{1,0:T(8,128)(2,1)S(1)}, u32[]{:S(2)}, u32[]{:S(2)}) collective-permute-start(bf16[1536,512]{1,0:T(8,128)(2,1)S(1)} %get-tuple-element.75), channel_id=1, source_target_pairs={{96,0},{25,1},{98,2},{27,3},{100,4},{29,5},{102,6},{31,7},{104,8},... | collective-permute-start | bytes 4718600 | tf_op jit(solution)/shard_map/ppermute | solution.py:53
  22.3 16.4 %collective-permute-start.6 = (bf16[528,512]{1,0:T(8,128)(2,1)S(1)}, bf16[528,512]{1,0:T(8,128)(2,1)S(1)}, u32[]{:S(2)}, u32[]{:S(2)}) collective-permute-start(bf16[528,512]{1,0:T(8,128)(2,1)S(1)} %get-tuple-element.66), channel_id=1, source_target_pairs={{24,0},{97,1},{26,2},{99,3},{28,4},{101,5},{30,6},{103,7},{0,8},{1... | collective-permute-start | bytes 1622024 | tf_op jit(solution)/shard_map/ppermute | solution.py:53
  23.8 14.9 %collective-permute-start.5 = (bf16[512,512]{1,0:T(8,128)(2,1)S(1)}, bf16[512,512]{1,0:T(8,128)(2,1)S(1)}, u32[]{:S(2)}, u32[]{:S(2)}) collective-permute-start(bf16[512,512]{1,0:T(8,128)(2,1)S(1)} %get-tuple-element.65), channel_id=1, source_target_pairs={{8,0},{33,1},{10,2},{35,3},{12,4},{37,5},{14,6},{39,7},{16,8},{41,... | collective-permute-start | bytes 1572872 | tf_op jit(solution)/shard_map/ppermute | solution.py:53
  38.7 20.4 %copy-start.6 = (s32[192,5,128]{2,0,1:T(8,128)S(1)}, s32[192,5,128]{2,0,1:T(8,128)}, u32[]{:S(2)}) copy-start(s32[192,5,128]{2,0,1:T(8,128)} %param.13) | copy-start | bytes 1474564
  39.6 8.8 %collective-permute-start.9 = (f32[8,512]{1,0:T(8,128)S(1)}, f32[8,512]{1,0:T(8,128)S(1)}, u32[]{:S(2)}, u32[]{:S(2)}) collective-permute-start(f32[8,512]{1,0:T(8,128)S(1)} %get-tuple-element.72), channel_id=1, source_target_pairs={{64,0},{17,1},{66,2},{19,3},{68,4},{21,5},{70,6},{23,7},{72,8},{25... | collective-permute-start | bytes 49160 | tf_op jit(solution)/shard_map/ppermute | solution.py:53
  41.9 6.5 %collective-permute-start.8 = (f32[8,512]{1,0:T(8,128)S(1)}, f32[8,512]{1,0:T(8,128)S(1)}, u32[]{:S(2)}, u32[]{:S(2)}) collective-permute-start(f32[8,512]{1,0:T(8,128)S(1)} %get-tuple-element.72), channel_id=1, source_target_pairs={{96,0},{25,1},{98,2},{27,3},{100,4},{29,5},{102,6},{31,7},{104,8},... | collective-permute-start | bytes 49160 | tf_op jit(solution)/shard_map/ppermute | solution.py:53
  43.8 4.6 %collective-permute-start.7 = (f32[8,512]{1,0:T(8,128)S(1)}, f32[8,512]{1,0:T(8,128)S(1)}, u32[]{:S(2)}, u32[]{:S(2)}) collective-permute-start(f32[8,512]{1,0:T(8,128)S(1)} %get-tuple-element.72), channel_id=1, source_target_pairs={{32,0},{9,1},{34,2},{11,3},{36,4},{13,5},{38,6},{15,7},{40,8},{17,... | collective-permute-start | bytes 49160 | tf_op jit(solution)/shard_map/ppermute | solution.py:53
  48.4 27.7 %collective-permute-start.12 = (bf16[2048,512]{1,0:T(8,128)(2,1)S(1)}, bf16[2048,512]{1,0:T(8,128)(2,1)S(1)}, u32[]{:S(2)}, u32[]{:S(2)}) collective-permute-start(bf16[2048,512]{1,0:T(8,128)(2,1)S(1)} %get-tuple-element.76), channel_id=1, source_target_pairs={{64,0},{17,1},{66,2},{19,3},{68,4},{21,5},{70,6},{23,7},{72,8},{25... | collective-permute-start | bytes 6291464 | tf_op jit(solution)/shard_map/ppermute | solution.py:53
  49.1 31.5 %collective-permute-start.13 = (bf16[512,512]{1,0:T(8,128)(2,1)S(1)}, bf16[512,512]{1,0:T(8,128)(2,1)S(1)}, u32[]{:S(2)}, u32[]{:S(2)}) collective-permute-start(bf16[512,512]{1,0:T(8,128)(2,1)S(1)} %get-tuple-element.81), channel_id=1, source_target_pairs={{32,0},{9,1},{34,2},{11,3},{36,4},{13,5},{38,6},{15,7},{40,8},{17,... | collective-permute-start | bytes 1572872 | tf_op jit(solution)/shard_map/ppermute | solution.py:53
  50.8 30.8 %collective-permute-start.14 = (bf16[512,512]{1,0:T(8,128)(2,1)S(1)}, bf16[512,512]{1,0:T(8,128)(2,1)S(1)}, u32[]{:S(2)}, u32[]{:S(2)}) collective-permute-start(bf16[512,512]{1,0:T(8,128)(2,1)S(1)} %get-tuple-element.82), channel_id=1, source_target_pairs={{96,0},{25,1},{98,2},{27,3},{100,4},{29,5},{102,6},{31,7},{104,8},... | collective-permute-start | bytes 1572872 | tf_op jit(solution)/shard_map/ppermute | solution.py:53
  51.2 1.2 collective-permute-start.15
  52.4 3.7 %collective-permute-start.16 = (f32[8,512]{1,0:T(8,128)S(1)}, f32[8,512]{1,0:T(8,128)S(1)}, u32[]{:S(2)}, u32[]{:S(2)}) collective-permute-start(f32[8,512]{1,0:T(8,128)S(1)} %add.41), channel_id=1, source_target_pairs={{0,2},{2,0},{4,6},{6,4},{1,3},{3,1},{5,7},{7,5},{8,10},{10,8},{12,... | collective-permute-start | bytes 49160 | tf_op jit(solution)/shard_map/ppermute | solution.py:60
  56.1 10.6 %collective-permute-start.17 = (f32[8,512]{1,0:T(8,128)S(1)}, f32[8,512]{1,0:T(8,128)S(1)}, u32[]{:S(2)}, u32[]{:S(2)}) collective-permute-start(f32[8,512]{1,0:T(8,128)S(1)} %add.42), channel_id=1, source_target_pairs={{0,4},{2,6},{4,0},{6,2},{1,5},{3,7},{5,1},{7,3},{8,12},{10,14},{12... | collective-permute-start | bytes 49160 | tf_op jit(solution)/shard_map/ppermute | solution.py:60
  66.7 14.9 %copy-start.1 = (f32[1024,512]{1,0:T(8,128)S(1)}, f32[1024,512]{1,0:T(8,128)}, u32[]{:S(2)}) copy-start(f32[1024,512]{1,0:T(8,128)} %refs_8_.1) | copy-start | bytes 6291460
  85.6 16.3 %collective-permute-start.19 = (bf16[1040,512]{1,0:T(8,128)(2,1)S(1)}, bf16[1040,512]{1,0:T(8,128)(2,1)S(1)}, u32[]{:S(2)}, u32[]{:S(2)}) collective-permute-start(bf16[1040,512]{1,0:T(8,128)(2,1)S(1)} %get-tuple-element.89.own.refs_4_), channel_id=1, source_target_pairs={{24,0},{97,1},{26,2},{99,3},{28,4},{101,5},{30,6},{103,7},{0,8},{1... | collective-permute-start | bytes 3194888 | tf_op jit(solution)/shard_map/ppermute | solution.py:53
  85.9 16.0 %collective-permute-start.18 = (bf16[1040,512]{1,0:T(8,128)(2,1)S(1)}, bf16[1040,512]{1,0:T(8,128)(2,1)S(1)}, u32[]{:S(2)}, u32[]{:S(2)}) collective-permute-start(bf16[1040,512]{1,0:T(8,128)(2,1)S(1)} %get-tuple-element.89.own.refs_4_), channel_id=1, source_target_pairs={{8,0},{33,1},{10,2},{35,3},{12,4},{37,5},{14,6},{39,7},{16,8},{41,... | collective-permute-start | bytes 3194888 | tf_op jit(solution)/shard_map/ppermute | solution.py:53
  102.8 27.1 %collective-permute-start.25 = (bf16[1536,512]{1,0:T(8,128)(2,1)S(1)}, bf16[1536,512]{1,0:T(8,128)(2,1)S(1)}, u32[]{:S(2)}, u32[]{:S(2)}) collective-permute-start(bf16[1536,512]{1,0:T(8,128)(2,1)S(1)} %get-tuple-element.99), channel_id=1, source_target_pairs={{32,0},{9,1},{34,2},{11,3},{36,4},{13,5},{38,6},{15,7},{40,8},{17,... | collective-permute-start | bytes 4718600 | tf_op jit(solution)/shard_map/ppermute | solution.py:53
  104.4 25.5 %collective-permute-start.26 = (bf16[1536,512]{1,0:T(8,128)(2,1)S(1)}, bf16[1536,512]{1,0:T(8,128)(2,1)S(1)}, u32[]{:S(2)}, u32[]{:S(2)}) collective-permute-start(bf16[1536,512]{1,0:T(8,128)(2,1)S(1)} %get-tuple-element.100), channel_id=1, source_target_pairs={{96,0},{25,1},{98,2},{27,3},{100,4},{29,5},{102,6},{31,7},{104,8},... | collective-permute-start | bytes 4718600 | tf_op jit(solution)/shard_map/ppermute | solution.py:53
  104.9 16.5 %collective-permute-start.21 = (bf16[528,512]{1,0:T(8,128)(2,1)S(1)}, bf16[528,512]{1,0:T(8,128)(2,1)S(1)}, u32[]{:S(2)}, u32[]{:S(2)}) collective-permute-start(bf16[528,512]{1,0:T(8,128)(2,1)S(1)} %get-tuple-element.91), channel_id=1, source_target_pairs={{24,0},{97,1},{26,2},{99,3},{28,4},{101,5},{30,6},{103,7},{0,8},{1... | collective-permute-start | bytes 1622024 | tf_op jit(solution)/shard_map/ppermute | solution.py:53
  106.2 15.0 %collective-permute-start.20 = (bf16[512,512]{1,0:T(8,128)(2,1)S(1)}, bf16[512,512]{1,0:T(8,128)(2,1)S(1)}, u32[]{:S(2)}, u32[]{:S(2)}) collective-permute-start(bf16[512,512]{1,0:T(8,128)(2,1)S(1)} %get-tuple-element.90), channel_id=1, source_target_pairs={{8,0},{33,1},{10,2},{35,3},{12,4},{37,5},{14,6},{39,7},{16,8},{41,... | collective-permute-start | bytes 1572872 | tf_op jit(solution)/shard_map/ppermute | solution.py:53
  122.2 7.3 %collective-permute-start.24 = (f32[8,512]{1,0:T(8,128)S(1)}, f32[8,512]{1,0:T(8,128)S(1)}, u32[]{:S(2)}, u32[]{:S(2)}) collective-permute-start(f32[8,512]{1,0:T(8,128)S(1)} %get-tuple-element.97), channel_id=1, source_target_pairs={{64,0},{17,1},{66,2},{19,3},{68,4},{21,5},{70,6},{23,7},{72,8},{25... | collective-permute-start | bytes 49160 | tf_op jit(solution)/shard_map/ppermute | solution.py:53
  123.6 5.9 %collective-permute-start.23 = (f32[8,512]{1,0:T(8,128)S(1)}, f32[8,512]{1,0:T(8,128)S(1)}, u32[]{:S(2)}, u32[]{:S(2)}) collective-permute-start(f32[8,512]{1,0:T(8,128)S(1)} %get-tuple-element.97), channel_id=1, source_target_pairs={{96,0},{25,1},{98,2},{27,3},{100,4},{29,5},{102,6},{31,7},{104,8},... | collective-permute-start | bytes 49160 | tf_op jit(solution)/shard_map/ppermute | solution.py:53
  126.1 3.7 %collective-permute-start.22 = (f32[8,512]{1,0:T(8,128)S(1)}, f32[8,512]{1,0:T(8,128)S(1)}, u32[]{:S(2)}, u32[]{:S(2)}) collective-permute-start(f32[8,512]{1,0:T(8,128)S(1)} %get-tuple-element.97), channel_id=1, source_target_pairs={{32,0},{9,1},{34,2},{11,3},{36,4},{13,5},{38,6},{15,7},{40,8},{17,... | collective-permute-start | bytes 49160 | tf_op jit(solution)/shard_map/ppermute | solution.py:53
  129.9 27.6 %collective-permute-start.27 = (bf16[2048,512]{1,0:T(8,128)(2,1)S(1)}, bf16[2048,512]{1,0:T(8,128)(2,1)S(1)}, u32[]{:S(2)}, u32[]{:S(2)}) collective-permute-start(bf16[2048,512]{1,0:T(8,128)(2,1)S(1)} %get-tuple-element.101), channel_id=1, source_target_pairs={{64,0},{17,1},{66,2},{19,3},{68,4},{21,5},{70,6},{23,7},{72,8},{25... | collective-permute-start | bytes 6291464 | tf_op jit(solution)/shard_map/ppermute | solution.py:53
  130.6 31.7 %collective-permute-start.28 = (bf16[512,512]{1,0:T(8,128)(2,1)S(1)}, bf16[512,512]{1,0:T(8,128)(2,1)S(1)}, u32[]{:S(2)}, u32[]{:S(2)}) collective-permute-start(bf16[512,512]{1,0:T(8,128)(2,1)S(1)} %get-tuple-element.106), channel_id=1, source_target_pairs={{32,0},{9,1},{34,2},{11,3},{36,4},{13,5},{38,6},{15,7},{40,8},{17,... | collective-permute-start | bytes 1572872 | tf_op jit(solution)/shard_map/ppermute | solution.py:53
  132.7 30.4 %collective-permute-start.29 = (bf16[512,512]{1,0:T(8,128)(2,1)S(1)}, bf16[512,512]{1,0:T(8,128)(2,1)S(1)}, u32[]{:S(2)}, u32[]{:S(2)}) collective-permute-start(bf16[512,512]{1,0:T(8,128)(2,1)S(1)} %get-tuple-element.107), channel_id=1, source_target_pairs={{96,0},{25,1},{98,2},{27,3},{100,4},{29,5},{102,6},{31,7},{104,8},... | collective-permute-start | bytes 1572872 | tf_op jit(solution)/shard_map/ppermute | solution.py:53
  132.7 1.3 collective-permute-start.30
  133.9 3.7 %collective-permute-start.31 = (f32[8,512]{1,0:T(8,128)S(1)}, f32[8,512]{1,0:T(8,128)S(1)}, u32[]{:S(2)}, u32[]{:S(2)}) collective-permute-start(f32[8,512]{1,0:T(8,128)S(1)} %add.47), channel_id=1, source_target_pairs={{0,2},{2,0},{4,6},{6,4},{1,3},{3,1},{5,7},{7,5},{8,10},{10,8},{12,... | collective-permute-start | bytes 49160 | tf_op jit(solution)/shard_map/ppermute | solution.py:60
  137.7 11.4 %collective-permute-start.32 = (f32[8,512]{1,0:T(8,128)S(1)}, f32[8,512]{1,0:T(8,128)S(1)}, u32[]{:S(2)}, u32[]{:S(2)}) collective-permute-start(f32[8,512]{1,0:T(8,128)S(1)} %add.48), channel_id=1, source_target_pairs={{0,4},{2,6},{4,0},{6,2},{1,5},{3,7},{5,1},{7,3},{8,12},{10,14},{12... | collective-permute-start | bytes 49160 | tf_op jit(solution)/shard_map/ppermute | solution.py:60
where the time goes:
time: 170 us; the launch traced here: 168 us
  waiting for transfers between devices  75.2 us (44%)
  starting transfers between devices  46.7 us (27%)
  Pallas kernels  43.3 us (25%)
  local copies, waits for them, and re-layouts  2.05 us (1%)
    ppermute x27, waiting for transfers between devices, fetch(): return lax.ppermute(value, ALL, pairs(first, second))  66.7 us
    ppermute x27, starting transfers between devices, fetch(): return lax.ppermute(value, ALL, pairs(first, second))  38.2 us
    pallas_call x6, Pallas kernels, run_tiles(): pl.pallas_call(functools.partial(tile_kernel, part, len(tables), earlier...  32 us
    ppermute x6, starting transfers between devices, sum_over_cols(): part = part + lax.ppermute(part, axis, [(i, i ^ step) for i in range(size)])  8.49 us
    ppermute x6, waiting for transfers between devices, sum_over_cols(): part = part + lax.ppermute(part, axis, [(i, i ^ step) for i in range(size)])  8.49 us
    pallas_call x1, Pallas kernels, ask(): pl.pallas_call(ask_kernel, out_shape=(jax.ShapeDtypeStruct((64,), i32), j...  3.87 us
    pallas_call x1, Pallas kernels, sort_tiles(): pl.pallas_call(sort_kernel, out_shape=(jax.ShapeDtypeStruct((SLOTS,), i32...  3.68 us
  transfers between devices with their start and end apart: 33, of which 22 were waited for; matrix products, arithmetic and copies ran while one was open for 0% of the time, Pallas kernels for 19%

commit v1 on v0

v1 whole, which is shorter than its diff:
```python
import functools

import jax
import jax.numpy as jnp
from jax import lax
from jax.experimental import pallas as pl
from jax.experimental.pallas import tpu as pltpu
from jax.sharding import Mesh
from jax.sharding import PartitionSpec as P

C = 512
BLOCK = 128
STEPS = 2
BPD = 8
SIDE = 4
CAP = 4
N_COLS = 8
NODES = 131072
UNIT = 1572864
PATTERNS = 192
TILES = 240
GROUP = 4
PARTS = 4
KEYS = PARTS * BPD
GROUPS = (TILES + KEYS * (GROUP - 1)) // GROUP + 2 * PARTS + 2
SLOTS = GROUPS * GROUP
LIST = SLOTS + GROUPS + 8
EMPTY = PATTERNS * 64
FLOOR = 0.001
STEP_SIZE = 0.3 / NODES
OWN_ROWS = BPD * BLOCK
SENT_ROWS = OWN_ROWS + 16
PICKED = SIDE * CAP
HALF_ROWS = OWN_ROWS // 2

ALL = ("rows_0", "rows_1", "cols_0", "cols_1")
VMEM = pl.BlockSpec(memory_space=pltpu.VMEM)
SMEM = pl.BlockSpec(memory_space=pltpu.SMEM)


def pairs(first, second):
    out = []
    for y in range(SIDE):
        for x in range(SIDE):
            for z in range(4):
                for core in range(2):
                    dx, dy = (first, second) if core == 0 else (second, first)
                    sy, sx = (y + dy) % SIDE, (x + dx) % SIDE
                    out.append((((sy * 4 + sx) * 4 + z) * 2 + core, ((y * 4 + x) * 4 + z) * 2 + core))
    return out


def fetch(value, first, second):
    return lax.ppermute(value, ALL, pairs(first, second))


def sum_over_cols(part):
    for axis, size in (("cols_1", 2), ("cols_0", 4)):
        step = 1
        while step < size:
            part = part + lax.ppermute(part, axis, [(i, i ^ step) for i in range(size)])
            step *= 2
    return part


OWNERS = (
    ((0, 1), (0, 2), (0, 3)),
    ((1, 0), (1, 1), (1, 2), (1, 3), (3, 0), (3, 1), (3, 2), (3, 3)),
    ((2, 0), (2, 1)),
    ((2, 2), (2, 3)),
)


def clear(ref, start, size, value):
    def body(i, _):
        for j in range(8):
            ref[start + 8 * i + j] = value
        return 0

    lax.fori_loop(0, size // 8, body, 0)


def ask_kernel(place, blocks, targets, count, home, requests, codes, rank, fill, base):
    first, second, core = place[0], place[1], place[2]
    clear(rank, 0, 128, -1)
    clear(fill, 0, 16, 0)
    clear(requests, 0, 64, 0)
    base[0] = 0
    for part, owners in enumerate(OWNERS):
        for i, (m, k) in enumerate(owners):
            base[m * SIDE + k] = part * 512 + i * CAP

    def note(t, _):
        slot = home[blocks[t]]
        row = slot >> 6
        local = slot & (BPD - 1)
        y, x = row >> 2, row & (SIDE - 1)
        owner_first = jnp.where(core == 0, x, y)
        owner_second = jnp.where(core == 0, y, x)
        k = (owner_first - first) & (SIDE - 1)
        m = (owner_second - second) & (SIDE - 1)
        pair = m * SIDE + k
        seen = rank[pair * BPD + local]
        held = fill[pair]
        mine = jnp.minimum(jnp.where(seen < 0, held, seen), CAP - 1)
        rank[pair * BPD + local] = mine
        fill[pair] = jnp.where(seen < 0, held + 1, held)
        requests[pair * CAP + mine] = local
        codes[t] = base[pair] + mine + targets[t] * 64
        return 0

    lax.fori_loop(0, count[0], note, 0)


def ask(place, blocks, targets, count, home):
    i32 = jnp.int32
    return pl.pallas_call(
        ask_kernel,
        out_shape=(jax.ShapeDtypeStruct((64,), i32), jax.ShapeDtypeStruct((TILES,), i32)),
        in_specs=[SMEM] * 5,
        out_specs=(SMEM,) * 2,
        scratch_shapes=[pltpu.SMEM((128,), i32), pltpu.SMEM((16,), i32), pltpu.SMEM((16,), i32)],
        compiler_params=pltpu.CompilerParams(vmem_limit_bytes=2 << 20),
        name="ask",
    )(place, blocks, targets, count, home)


def sort_kernel(codes, pattern_ids, count, lists, per_key):
    clear(per_key, 0, KEYS, 0)
    clear(lists, 0, SLOTS, EMPTY)
    clear(lists, SLOTS, GROUPS, 0)

    def tally(t, _):
        key = codes[t] >> 6
        per_key[key] = per_key[key] + 1
        return 0

    lax.fori_loop(0, count[0], tally, 0)
    group = jnp.int32(0)
    for part in range(PARTS):
        lists[SLOTS + GROUPS + part] = group
        start = group
        for target in range(BPD):
            key = part * BPD + target
            size = (per_key[key] + GROUP - 1) >> 2
            per_key[key] = group * GROUP
            group = group + size
        group = start + jnp.maximum(2, (group - start + 1) & -2)
    lists[SLOTS + GROUPS + PARTS] = group

    def put(t, _):
        code = codes[t]
        key = code >> 6
        at = per_key[key]
        per_key[key] = at + 1
        lists[at] = pattern_ids[t] * 64 + (code & 63)
        lists[SLOTS + (at >> 2)] = key & (BPD - 1)
        return 0

    lax.fori_loop(0, count[0], put, 0)


def sort_tiles(codes, pattern_ids, count):
    i32 = jnp.int32
    return pl.pallas_call(
        sort_kernel,
        out_shape=jax.ShapeDtypeStruct((LIST,), i32),
        in_specs=[SMEM] * 3,
        out_specs=SMEM,
        scratch_shapes=[pltpu.SMEM((KEYS,), i32)],
        compiler_params=pltpu.CompilerParams(vmem_limit_bytes=2 << 20),
        name="sort_tiles",
    )(codes, pattern_ids, count)


def sum_rows(total):
    high = total.astype(jnp.bfloat16).astype(jnp.float32)
    rest = total - high
    middle = rest.astype(jnp.bfloat16).astype(jnp.float32)
    low = rest - middle
    row = lax.broadcasted_iota(jnp.int32, (16, C), 0)
    out = jnp.where(row == 0, high, jnp.where(row == 1, middle, jnp.where(row == 2, low, 0.0)))
    return out.astype(jnp.bfloat16)


SENT = tuple(
    jax.ShapeDtypeStruct((rows, C), jnp.bfloat16) for rows in (SENT_ROWS, HALF_ROWS + 16, HALF_ROWS + 16)
)


def put_block(j, rows, sent, low, high):
    sent[pl.ds(j * BLOCK, BLOCK), :] = rows
    half, at = (low, j) if j < BPD // 2 else (high, j - BPD // 2)
    half[pl.ds(at * BLOCK, BLOCK), :] = rows


def put_sums(total, sent, low, high):
    rows = sum_rows(total)
    sent[pl.ds(OWN_ROWS, 16), :] = rows
    for half in (low, high):
        half[pl.ds(HALF_ROWS, 16), :] = rows


def first_kernel(current, sent, low, high):
    total = jnp.zeros((8, C), jnp.float32)
    for j in range(BPD):
        rows = current[pl.ds(j * BLOCK, BLOCK), :]
        put_block(j, rows.astype(jnp.bfloat16), sent, low, high)
        total = total + jnp.sum(rows.reshape(BLOCK // 8, 8, C), axis=0)
    put_sums(jnp.sum(total, axis=0, keepdims=True), sent, low, high)


def first(current):
    return pl.pallas_call(
        first_kernel,
        out_shape=SENT,
        in_specs=[VMEM],
        out_specs=(VMEM,) * 3,
        compiler_params=pltpu.CompilerParams(vmem_limit_bytes=20 << 20),
        name="first",
    )(current)


def move(table, local, out, at):
    rows = pl.ds(pl.multiple_of(local * BLOCK, BLOCK), BLOCK)
    out[pl.ds(at * BLOCK, BLOCK), :] = table[rows, :]


def pick_kernel(
    asked, wanted, own, low1, high1, low2, high2, low3, high3,
    near, out1, out3, out2a, out2b, line, far1, far2, far3,
):
    for low, high, far in ((low1, high1, far1), (low2, high2, far2), (low3, high3, far3)):
        far[pl.ds(0, HALF_ROWS), :] = low[pl.ds(0, HALF_ROWS), :]
        far[pl.ds(HALF_ROWS, HALF_ROWS + 16), :] = high[...]
    tables = (own, far1, far2, far3)
    for m, out in ((1, out1), (3, out3)):
        for k, table in enumerate(tables):
            for r in range(CAP):
                move(table, asked[m - 1, k * CAP + r], out, k * CAP + r)
    for k, table in enumerate(tables):
        out, at = (out2a, k) if k < 2 else (out2b, k - 2)
        for r in range(CAP):
            move(table, asked[1, k * CAP + r], out, at * CAP + r)
            if k > 0:
                move(table, wanted[k * CAP + r], near, (k - 1) * CAP + r)
    rows = sum(t[pl.ds(OWN_ROWS, 16), :].astype(jnp.float32) for t in tables)
    sums = jnp.sum(rows, axis=0, keepdims=True)
    line[...] = jnp.broadcast_to(sums, (8, C))
    for out in (out1, out3):
        out[pl.ds(PICKED * BLOCK, 16), :] = sum_rows(sums)


def pick(asked, wanted, own, *far):
    b16 = jnp.bfloat16
    shape = lambda rows: jax.ShapeDtypeStruct((rows, C), b16)
    return pl.pallas_call(
        pick_kernel,
        out_shape=(
            shape(3 * CAP * BLOCK),
            shape(PICKED * BLOCK + 16),
            shape(PICKED * BLOCK + 16),
            shape(2 * CAP * BLOCK),
            shape(2 * CAP * BLOCK),
            jax.ShapeDtypeStruct((8, C), jnp.float32),
        ),
        in_specs=[SMEM] * 2 + [VMEM] * 7,
        out_specs=(VMEM,) * 6,
        scratch_shapes=[pltpu.VMEM((SENT_ROWS, C), b16)] * 3,
        compiler_params=pltpu.CompilerParams(vmem_limit_bytes=20 << 20),
        name="pick",
    )(asked, wanted, own, *far)


def tile_kernel(part, table_count, resume, finish, *refs):
    refs = list(refs)
    lists, words, own = refs[:3]
    tables = refs[3 : 3 + table_count]
    refs = refs[3 + table_count :]
    if resume:
        earlier = refs.pop(0)
    if finish:
        current, chain, cross, fresh = refs[:4]
        refs = refs[4:]
        if finish == "more":
            sent = refs[:3]
            refs = refs[3:]
    total, score_a, score_b, bits = refs[:4]

    row = lax.broadcasted_iota(jnp.int32, (BLOCK, BLOCK), 0)
    bits[...] = lax.shift_left(jnp.ones_like(row), lax.rem(row, 30))
    total[...] = earlier[...] if resume else jnp.zeros_like(total)
    sub = lax.broadcasted_iota(jnp.int32, (8, BLOCK), 0)
    if table_count == 1:
        held = tables[0]
    else:
        held = refs[4]
        at = 0
        for table in tables:
            held[pl.ds(at, PICKED * BLOCK), :] = table[pl.ds(0, PICKED * BLOCK), :]
            at += PICKED * BLOCK

    def rows_of(index):
        return pl.ds(pl.multiple_of(index * BLOCK, BLOCK), BLOCK)

    def word_rows(pattern):
        rows = []
        for v in range(BLOCK // 8):
            low, high = 8 * v // 30, (8 * v + 7) // 30
            chunk = jnp.broadcast_to(words[pattern, low : low + 1, :], (8, BLOCK))
            if high != low:
                other = jnp.broadcast_to(words[pattern, high : high + 1, :], (8, BLOCK))
                chunk = jnp.where(sub + 8 * v < 30 * high, chunk, other)
            rows.append(chunk)
        return jnp.concatenate(rows, axis=0)

    def remote(group, i):
        return held[rows_of(lists[group * GROUP + i] & 63), :]

    def score(group, out):
        mine = own[rows_of(lists[SLOTS + group]), :]
        for i in range(GROUP):
            out[:, i * BLOCK : (i + 1) * BLOCK] = lax.dot_general(
                mine,
                remote(group, i),
                (((1,), (1,)), ((), ())),
                preferred_element_type=jnp.float32,
            )

    def add(group, scores):
        weights = []
        for i in range(GROUP):
            packed = word_rows(lists[group * GROUP + i] >> 6)
            negative = jnp.minimum(scores[:, i * BLOCK : (i + 1) * BLOCK] * (-1.0 / UNIT), -FLOOR)
            weight = 1.0 / (1.0 - jnp.exp(negative))
            linked = (packed & bits[...]) != 0
            weights.append(jnp.where(linked, weight, 0.0).astype(jnp.bfloat16))
        total[rows_of(lists[SLOTS + group]), :] += jnp.dot(
            jnp.concatenate(weights, axis=1),
            jnp.concatenate([remote(group, i) for i in range(GROUP)], axis=0),
            preferred_element_type=jnp.float32,
        )

    start, stop = lists[SLOTS + GROUPS + part], lists[SLOTS + GROUPS + part + 1]
    score(start, score_a)

    def two(i, _):
        group = start + 2 * i
        score(group + 1, score_b)
        add(group, score_a)
        score(jnp.minimum(group + 2, stop - 1), score_a)
        add(group + 1, score_b)
        return 0

    lax.fori_loop(0, (stop - start) >> 1, two, 0)

    if finish:
        col_sums = chain[0:1, :] + cross[4:5, :]
        moved_sums = jnp.zeros((8, C), jnp.float32)
        for j in range(BPD):
            at = pl.ds(j * BLOCK, BLOCK)
            moved = jnp.maximum(current[at, :] + STEP_SIZE * (total[at, :] - col_sums), 0.0)
            fresh[at, :] = moved
            if finish == "more":
                put_block(j, moved.astype(jnp.bfloat16), *sent)
                moved_sums = moved_sums + jnp.sum(moved.reshape(BLOCK // 8, 8, C), axis=0)
        if finish == "more":
            put_sums(jnp.sum(moved_sums, axis=0, keepdims=True), *sent)


def run_tiles(name, part, lists, words, own, tables, earlier=None, current=None, sums=(), finish=""):
    f32 = jnp.float32
    blocks = jax.ShapeDtypeStruct((OWN_ROWS, C), f32)
    args = [lists, words, own, *tables]
    specs = [SMEM] + [VMEM] * (2 + len(tables))
    scratch = []
    out = [blocks]
    if earlier is not None:
        args.append(earlier)
        specs.append(VMEM)
    if finish:
        args += [current, *sums]
        specs += [VMEM] * 3
        scratch.append(pltpu.VMEM((OWN_ROWS, C), f32))
        if finish == "more":
            out += SENT
    scratch += [
        pltpu.VMEM((BLOCK, GROUP * BLOCK), f32),
        pltpu.VMEM((BLOCK, GROUP * BLOCK), f32),
        pltpu.VMEM((BLOCK, BLOCK), jnp.int32),
    ]
    if len(tables) > 1:
        scratch.append(pltpu.VMEM((len(tables) * PICKED * BLOCK, C), jnp.bfloat16))
    return pl.pallas_call(
        functools.partial(tile_kernel, part, len(tables), earlier is not None, finish),
        out_shape=tuple(out),
        in_specs=specs,
        out_specs=(VMEM,) * len(out),
        scratch_shapes=scratch,
        compiler_params=pltpu.CompilerParams(vmem_limit_bytes=24 << 20),
        name=name,
    )(*args)


def line_sums(line, side1, side3):
    rows = sum(t[PICKED * BLOCK :].astype(jnp.float32) for t in (side1, side3))
    beside = jnp.sum(rows, axis=0, keepdims=True)
    return line + jnp.where(jnp.arange(8)[:, None] < 4, beside, 0.0)


def per_device(affiliations, tile_block, tile_target, tile_pattern, tile_count, block_home, patterns):
    y, x = lax.axis_index("rows_0"), lax.axis_index("rows_1")
    core = lax.axis_index("cols_1")
    place = jnp.stack([jnp.where(core == 0, x, y), jnp.where(core == 0, y, x), core])
    current = affiliations
    own, low, high = first(current)
    requests, codes = ask(
        place.astype(jnp.int32), tile_block[0], tile_target[0], tile_count, block_home
    )
    requests = requests.reshape(SIDE, PICKED)
    asked = jnp.stack([fetch(requests[m], 0, SIDE - m) for m in (1, 2, 3)])
    words = jnp.concatenate([patterns, jnp.zeros((1, *patterns.shape[1:]), jnp.int32)], axis=0)

    lists = sort_tiles(codes, tile_pattern[0], tile_count)
    for step in range(STEPS):
        low1, high3 = fetch(low, 1, 0), fetch(high, 3, 0)
        high1, low3 = fetch(high, 1, 0), fetch(low, 3, 0)
        low2, high2 = fetch(low1, 1, 0), fetch(high3, 3, 0)
        lists, low2, high2 = lax.optimization_barrier((lists, low2, high2))
        near, out1, out3, out2a, out2b, line = pick(
            asked, requests[0], own, low1, high1, low2, high2, low3, high3
        )
        side1, side3 = fetch(out1, 0, 1), fetch(out3, 0, 3)
        far_a, far_b = fetch(out2a, 0, 2), fetch(out2b, 0, 2)
        (total,) = run_tiles("near", 0, lists, words, own, (near,))
        total, side1, side3 = lax.optimization_barrier((total, side1, side3))
        chain = sum_over_cols(line_sums(line, side1, side3))
        cross = fetch(chain, 2, 2)
        (total,) = run_tiles("sides", 1, lists, words, own, (side1, side3), total)
        (total,) = run_tiles("across", 2, lists, words, own, (far_a,), total)
        total, far_b = lax.optimization_barrier((total, far_b))
        finish = "more" if step < STEPS - 1 else "end"
        current, *own_next = run_tiles(
            "late", 3, lists, words, own, (far_b,), total, current, (chain, cross), finish
        )
        if own_next:
            own, low, high = own_next
    return current


def solution(mesh):
    torus = Mesh(mesh.devices.reshape(4, 4, 4, 2), ALL)
    return jax.shard_map(
        per_device,
        mesh=torus,
        in_specs=(P(ALL, None), P(ALL, None), P(ALL, None), P(ALL, None), P(ALL), P(), P()),
        out_specs=P(ALL, None),
        check_vma=False,
    )
```

time: 170 us -> 227 us (1.34)
  the two profiles are of different devices: /device:TPU:32 before, /device:TPU:4 now
where the time goes in v1:
time: 227 us; the launch traced here: 226 us
  waiting for transfers between devices  120 us (53%)
  Pallas kernels  51.2 us (23%)
  starting transfers between devices  51 us (22%)
    ppermute x25, waiting for transfers between devices, fetch(): return lax.ppermute(value, ALL, pairs(first, second))  110 us
    ppermute x25, starting transfers between devices, fetch(): return lax.ppermute(value, ALL, pairs(first, second))  40.3 us
    pallas_call x8, Pallas kernels, run_tiles(): pl.pallas_call(functools.partial(tile_kernel, part, len(tables), earlier...  38.6 us
    ppermute x6, starting transfers between devices, sum_over_cols(): part = part + lax.ppermute(part, axis, [(i, i ^ step) for i in range(size)])  10.7 us
    ppermute x6, waiting for transfers between devices, sum_over_cols(): part = part + lax.ppermute(part, axis, [(i, i ^ step) for i in range(size)])  9.81 us
  transfers between devices with their start and end apart: 31, of which 18 were waited for; matrix products, arithmetic and copies ran while one was open for 0% of the time, Pallas kernels for 17%

profile of v1, /device:TPU:4, one launch (start us, length us, event | category | flops | bytes accessed | tf_op | source)
XLA Modules:
  0.0 225.7 jit_solution(18030084569391968097)
XLA Ops:
  0.0 1.6 copy-done
  1.6 1.1 first.1
  2.7 0.5 collective-permute-start
  3.3 1.5 collective-permute-start.2
  4.8 7.5 %collective-permute-done.low1 = bf16[528,512]{1,0:T(8,128)(2,1)S(1)} collective-permute-done((bf16[528,512]{1,0:T(8,128)(2,1)}, bf16[528,512]{1,0:T(8,128)(2,1)S(1)}, u32[]{:S(2)}, u32[]{:S(2)}) %collective-permute-start) | collective-permute-done | bytes 540704 | tf_op jit(solution)/shard_map/ppermute | solution.py:54
  12.3 0.5 collective-permute-start.1
  12.8 1.9 collective-permute-start.3
  14.7 3.2 %collective-permute-start.8 = (bf16[528,512]{1,0:T(8,128)(2,1)}, bf16[528,512]{1,0:T(8,128)(2,1)}, u32[]{:S(2)}, u32[]{:S(2)}) collective-permute-start(bf16[528,512]{1,0:T(8,128)(2,1)} %get-tuple-element.43), channel_id=1, source_target_pairs={{24,0},{97,1},{26,2},{99,3},{28,4},{101,5},{30,6},{103,7},{0,8},{1... | collective-permute-start | bytes 1622024 | tf_op jit(solution)/shard_map/ppermute | solution.py:54
  18.6 0.1 pad_add_fusion.1.place
  18.7 4.1 %ask.1 = (s32[64]{0:T(128)S(1)}, s32[240]{0:T(256)S(1)}) custom-call(s32[3]{0:T(128)S(1)} %pad_add_fusion.1.place, s32[240]{0:T(256)S(1)} %bitcast.9, s32[240]{0:T(256)S(1)} %bitcast.10, s32[1]{0:T(128)S(6)} %copy.9.count, s32[1024]{0:T(1024)S(1)} %copy-done.2), custom_call_target="tpu_custom_call" | custom-call | tf_op jit(solution)/shard_map/ask/pallas_call | solution.py:117
  22.8 0.1 fusion
  22.9 2.4 %collective-permute-start.6 = (s32[16]{0:T(128)S(1)}, s32[16]{0:T(128)S(1)}, u32[]{:S(2)}, u32[]{:S(2)}) collective-permute-start(s32[16]{0:T(128)S(1)} %get-tuple-element.80), channel_id=1, source_target_pairs={{32,0},{9,1},{34,2},{11,3},{36,4},{13,5},{38,6},{15,7},{40,8},{17,... | collective-permute-start | bytes 200 | tf_op jit(solution)/shard_map/ppermute | solution.py:54
  25.2 1.3 collective-permute-done.6
  26.5 2.6 %collective-permute-start.5 = (s32[16]{0:T(128)S(1)}, s32[16]{0:T(128)S(1)}, u32[]{:S(2)}, u32[]{:S(2)}) collective-permute-start(s32[16]{0:T(128)S(1)} %get-tuple-element.81), channel_id=1, source_target_pairs={{64,0},{17,1},{66,2},{19,3},{68,4},{21,5},{70,6},{23,7},{72,8},{25... | collective-permute-start | bytes 200 | tf_op jit(solution)/shard_map/ppermute | solution.py:54
  29.1 2.5 %collective-permute-done.5 = s32[16]{0:T(128)S(1)} collective-permute-done((s32[16]{0:T(128)S(1)}, s32[16]{0:T(128)S(1)}, u32[]{:S(2)}, u32[]{:S(2)}) %collective-permute-start.5) | collective-permute-done | bytes 96 | tf_op jit(solution)/shard_map/ppermute | solution.py:54
  31.6 1.0 collective-permute-start.4
  32.5 4.0 %sort_tiles.1.refs_0_ = s32[478]{0:T(512)S(1)} custom-call(s32[240]{0:T(256)S(1)} %get-tuple-element.42.codes, s32[240]{0:T(256)S(1)} %bitcast.11, s32[1]{0:T(128)S(6)} %copy.9.count), custom_call_target="tpu_custom_call" | custom-call | tf_op jit(solution)/shard_map/sort_tiles/pallas_call | solution.py:165
  36.5 0.1 collective-permute-done.4
  36.7 2.0 pick.2
  38.7 2.1 collective-permute-start.10
  40.8 3.4 %collective-permute-start.9 = (bf16[1024,512]{1,0:T(8,128)(2,1)S(1)}, bf16[1024,512]{1,0:T(8,128)(2,1)S(1)}, u32[]{:S(2)}, u32[]{:S(2)}) collective-permute-start(bf16[1024,512]{1,0:T(8,128)(2,1)S(1)} %get-tuple-element.50), channel_id=1, source_target_pairs={{64,0},{17,1},{66,2},{19,3},{68,4},{21,5},{70,6},{23,7},{72,8},{25... | collective-permute-start | bytes 3145736 | tf_op jit(solution)/shard_map/ppermute | solution.py:54
  44.2 0.1 collective-permute-start.12
  44.3 0.3 copy.8
  44.7 3.4 %near.2.refs_5_ = f32[1024,512]{1,0:T(8,128)S(1)} custom-call(s32[478]{0:T(512)S(1)} %sort_tiles.1.refs_0_, s32[193,5,128]{2,1,0:T(8,128)S(1)} %concatenate.3.refs_1_, bf16[1040,512]{1,0:T(8,128)(2,1)S(1)} %get-tuple-element.46.own.refs_2_, bf16[1536,512]{1,0:T(8,128)(2,1)S(1)} %get-tuple-element.51.refs_3_), custom_call_target="tpu_custom_call" | custom-call | tf_op jit(solution)/shard_map/near/pallas_call | solution.py:394
  48.1 38.9 %collective-permute-done.10.refs_3_ = bf16[2064,512]{1,0:T(8,128)(2,1)S(1)} collective-permute-done((bf16[2064,512]{1,0:T(8,128)(2,1)S(1)}, bf16[2064,512]{1,0:T(8,128)(2,1)S(1)}, u32[]{:S(2)}, u32[]{:S(2)}) %collective-permute-start.10) | collective-permute-done | bytes 2113568 | tf_op jit(solution)/shard_map/ppermute | solution.py:54
  87.0 0.1 select_add_fusion.1
  87.1 1.2 collective-permute-done.13
  88.3 0.1 fusion.2
  88.4 2.2 collective-permute-start.14
  90.6 1.7 collective-permute-done.14
  92.3 3.4 %collective-permute-start.15 = (f32[8,512]{1,0:T(8,128)S(1)}, f32[8,512]{1,0:T(8,128)S(1)}, u32[]{:S(2)}, u32[]{:S(2)}) collective-permute-start(f32[8,512]{1,0:T(8,128)S(1)} %add.35), channel_id=1, source_target_pairs={{0,4},{2,6},{4,0},{6,2},{1,5},{3,7},{5,1},{7,3},{8,12},{10,14},{12... | collective-permute-start | bytes 49160 | tf_op jit(solution)/shard_map/ppermute | solution.py:61
  95.7 1.9 collective-permute-done.15
  97.6 5.8 %collective-permute-start.16 = (f32[8,512]{1,0:T(8,128)S(1)}, f32[8,512]{1,0:T(8,128)S(1)}, u32[]{:S(2)}, u32[]{:S(2)}) collective-permute-start(f32[8,512]{1,0:T(8,128)S(1)} %add.36.refs_6_), channel_id=1, source_target_pairs={{80,0},{81,1},{82,2},{83,3},{84,4},{85,5},{86,6},{87,7},{88,8},{89... | collective-permute-start | bytes 49160 | tf_op jit(solution)/shard_map/ppermute | solution.py:54
  103.4 7.8 %sides.2.refs_4_ = f32[1024,512]{1,0:T(8,128)S(1)} custom-call(s32[478]{0:T(512)S(1)} %sort_tiles.1.refs_0_, s32[193,5,128]{2,1,0:T(8,128)S(1)} %concatenate.3.refs_1_, bf16[1040,512]{1,0:T(8,128)(2,1)S(1)} %get-tuple-element.46.own.refs_2_, bf16[2064,512]{1,0:T(8,128)(2,1)S(1)} %collective-permute-done.10.refs_3_, ...), custom_call_target="tpu_custom_call" | custom-call | tf_op jit(solution)/shard_map/sides/pallas_call | solution.py:394
  111.2 3.4 %across.2.refs_4_ = f32[1024,512]{1,0:T(8,128)S(1)} custom-call(s32[478]{0:T(512)S(1)} %sort_tiles.1.refs_0_, s32[193,5,128]{2,1,0:T(8,128)S(1)} %concatenate.3.refs_1_, bf16[1040,512]{1,0:T(8,128)(2,1)S(1)} %get-tuple-element.46.own.refs_2_, bf16[1024,512]{1,0:T(8,128)(2,1)S(1)} %collective-permute-done.9.refs_3_, f32[1024,512]{1,0:T(8,128)S(1)} %sides.2.refs_4_), custom_call_target="tpu_custom_call" | custom-call | tf_op jit(solution)/shard_map/across/pallas_call | solution.py:394
  114.7 3.9 %late.2 = (f32[1024,512]{1,0:T(8,128)S(1)}, bf16[1040,512]{1,0:T(8,128)(2,1)S(1)}, bf16[528,512]{1,0:T(8,128)(2,1)S(1)}, bf16[528,512]{1,0:T(8,128)(2,1)S(1)}) custom-call(s32[478]{0:T(512)S(1)} %sort_tiles.1.refs_0_, s32[193,5,128]{2,1,0:T(8,128)S(1)} %concatenate.3.refs_1_, bf16[1040,512]{1,0:T(8,128)(2,1)S(1)} %get-tuple-element.46.own.refs_2_, ...), custom_call_target="tpu_custom_call" | custom-call | tf_op jit(solution)/shard_map/late/pallas_call | solution.py:394
  118.6 0.1 collective-permute-start.17
  118.7 2.0 collective-permute-start.19
  120.7 7.3 %collective-permute-done.17.low1 = bf16[528,512]{1,0:T(8,128)(2,1)S(1)} collective-permute-done((bf16[528,512]{1,0:T(8,128)(2,1)S(1)}, bf16[528,512]{1,0:T(8,128)(2,1)S(1)}, u32[]{:S(2)}, u32[]{:S(2)}) %collective-permute-start.17) | collective-permute-done | bytes 540704 | tf_op jit(solution)/shard_map/ppermute | solution.py:54
  128.0 0.3 collective-permute-done.19.high3
  128.3 1.8 collective-permute-start.20
  130.0 1.2 collective-permute-start.22
  131.2 0.8 collective-permute-start.21
  132.1 5.3 %collective-permute-done.18.low2 = bf16[528,512]{1,0:T(8,128)(2,1)S(1)} collective-permute-done((bf16[528,512]{1,0:T(8,128)(2,1)S(1)}, bf16[528,512]{1,0:T(8,128)(2,1)S(1)}, u32[]{:S(2)}, u32[]{:S(2)}) %collective-permute-start.18) | collective-permute-done | bytes 540704 | tf_op jit(solution)/shard_map/ppermute | solution.py:54
  137.4 0.3 collective-permute-done.20.high2
  137.6 5.8 %collective-permute-done.22.low3 = bf16[528,512]{1,0:T(8,128)(2,1)S(1)} collective-permute-done((bf16[528,512]{1,0:T(8,128)(2,1)S(1)}, bf16[528,512]{1,0:T(8,128)(2,1)S(1)}, u32[]{:S(2)}, u32[]{:S(2)}) %collective-permute-start.22) | collective-permute-done | bytes 540704 | tf_op jit(solution)/shard_map/ppermute | solution.py:54
  143.4 1.3 pick.3
  144.7 0.1 collective-permute-start.24
  144.8 2.0 collective-permute-start.25
  146.8 3.5 %collective-permute-start.26 = (bf16[1024,512]{1,0:T(8,128)(2,1)S(1)}, bf16[1024,512]{1,0:T(8,128)(2,1)S(1)}, u32[]{:S(2)}, u32[]{:S(2)}) collective-permute-start(bf16[1024,512]{1,0:T(8,128)(2,1)S(1)} %get-tuple-element.74), channel_id=1, source_target_pairs={{64,0},{17,1},{66,2},{19,3},{68,4},{21,5},{70,6},{23,7},{72,8},{25... | collective-permute-start | bytes 3145736 | tf_op jit(solution)/shard_map/ppermute | solution.py:54
  150.4 3.5 %near.3.refs_5_ = f32[1024,512]{1,0:T(8,128)S(1)} custom-call(s32[478]{0:T(512)S(1)} %sort_tiles.1.refs_0_, s32[193,5,128]{2,1,0:T(8,128)S(1)} %concatenate.3.refs_1_, bf16[1040,512]{1,0:T(8,128)(2,1)S(1)} %get-tuple-element.64.own.refs_2_, bf16[1536,512]{1,0:T(8,128)(2,1)S(1)} %get-tuple-element.68.refs_3_), custom_call_target="tpu_custom_call" | custom-call | tf_op jit(solution)/shard_map/near/pallas_call | solution.py:394
  153.8 17.2 %collective-permute-done.24.refs_3_ = bf16[2064,512]{1,0:T(8,128)(2,1)S(1)} collective-permute-done((bf16[2064,512]{1,0:T(8,128)(2,1)S(1)}, bf16[2064,512]{1,0:T(8,128)(2,1)S(1)}, u32[]{:S(2)}, u32[]{:S(2)}) %collective-permute-start.24) | collective-permute-done | bytes 2113568 | tf_op jit(solution)/shard_map/ppermute | solution.py:54
  171.0 23.8 %collective-permute-done.25.refs_4_ = bf16[2064,512]{1,0:T(8,128)(2,1)S(1)} collective-permute-done((bf16[2064,512]{1,0:T(8,128)(2,1)S(1)}, bf16[2064,512]{1,0:T(8,128)(2,1)S(1)}, u32[]{:S(2)}, u32[]{:S(2)}) %collective-permute-start.25) | collective-permute-done | bytes 2113568 | tf_op jit(solution)/shard_map/ppermute | solution.py:54
  194.8 0.1 select_add_fusion
  194.9 1.2 collective-permute-done.27
  196.1 0.1 fusion.1
  196.2 1.6 collective-permute-start.28
  197.8 2.1 collective-permute-done.28
  199.9 3.5 %collective-permute-start.29 = (f32[8,512]{1,0:T(8,128)S(1)}, f32[8,512]{1,0:T(8,128)S(1)}, u32[]{:S(2)}, u32[]{:S(2)}) collective-permute-start(f32[8,512]{1,0:T(8,128)S(1)} %add.40), channel_id=1, source_target_pairs={{0,4},{2,6},{4,0},{6,2},{1,5},{3,7},{5,1},{7,3},{8,12},{10,14},{12... | collective-permute-start | bytes 49160 | tf_op jit(solution)/shard_map/ppermute | solution.py:61
  203.4 1.7 collective-permute-done.29
  205.2 3.8 %collective-permute-start.30 = (f32[8,512]{1,0:T(8,128)S(1)}, f32[8,512]{1,0:T(8,128)S(1)}, u32[]{:S(2)}, u32[]{:S(2)}) collective-permute-start(f32[8,512]{1,0:T(8,128)S(1)} %add.41.refs_6_), channel_id=1, source_target_pairs={{80,0},{81,1},{82,2},{83,3},{84,4},{85,5},{86,6},{87,7},{88,8},{89... | collective-permute-start | bytes 49160 | tf_op jit(solution)/shard_map/ppermute | solution.py:54
  208.9 8.0 %sides.3.refs_4_ = f32[1024,512]{1,0:T(8,128)S(1)} custom-call(s32[478]{0:T(512)S(1)} %sort_tiles.1.refs_0_, s32[193,5,128]{2,1,0:T(8,128)S(1)} %concatenate.3.refs_1_, bf16[1040,512]{1,0:T(8,128)(2,1)S(1)} %get-tuple-element.64.own.refs_2_, bf16[2064,512]{1,0:T(8,128)(2,1)S(1)} %collective-permute-done.24.refs_3_, ...), custom_call_target="tpu_custom_call" | custom-call | tf_op jit(solution)/shard_map/sides/pallas_call | solution.py:394
  217.0 3.5 %across.3.refs_4_ = f32[1024,512]{1,0:T(8,128)S(1)} custom-call(s32[478]{0:T(512)S(1)} %sort_tiles.1.refs_0_, s32[193,5,128]{2,1,0:T(8,128)S(1)} %concatenate.3.refs_1_, bf16[1040,512]{1,0:T(8,128)(2,1)S(1)} %get-tuple-element.64.own.refs_2_, bf16[1024,512]{1,0:T(8,128)(2,1)S(1)} %collective-permute-done.23.refs_3_, f32[1024,512]{1,0:T(8,128)S(1)} %sides.3.refs_4_), custom_call_target="tpu_custom_call" | custom-call | tf_op jit(solution)/shard_map/across/pallas_call | solution.py:394
  220.5 5.2 %late.3 = f32[1024,512]{1,0:T(8,128)} custom-call(s32[478]{0:T(512)S(1)} %sort_tiles.1.refs_0_, s32[193,5,128]{2,1,0:T(8,128)S(1)} %concatenate.3.refs_1_, bf16[1040,512]{1,0:T(8,128)(2,1)S(1)} %get-tuple-element.64.own.refs_2_, bf16[1024,512]{1,0:T(8,128)(2,1)S(1)} %collective-permute-done.26.refs_3_, f32[1024,512]{1,0:T(8,128)S(1)} %across.3.refs_4_, ...), custom_call_target="tpu_custom_call" | custom-call | tf_op jit(solution)/shard_map/late/pallas_call | solution.py:394
  (41 shorter events, 0.3 us)
Async XLA Ops:
  0.0 1.6 copy-start
  1.6 17.1 %copy-start.2 = (s32[1024]{0:T(1024)S(1)}, s32[1024]{0:T(1024)}, u32[]{:S(2)}) copy-start(s32[1024]{0:T(1024)} %home.1) | copy-start | bytes 12292
  1.6 17.1 %copy-start.3 = (s32[1,240]{1,0:T(1,128)S(1)}, s32[1,240]{1,0:T(1,128)}, u32[]{:S(2)}) copy-start(s32[1,240]{1,0:T(1,128)} %param.8) | copy-start | bytes 2884
  1.6 17.1 %copy-start.4 = (s32[1,240]{1,0:T(1,128)S(1)}, s32[1,240]{1,0:T(1,128)}, u32[]{:S(2)}) copy-start(s32[1,240]{1,0:T(1,128)} %param.9) | copy-start | bytes 2884
  1.6 30.9 %copy-start.5 = (s32[1,240]{1,0:T(1,128)S(1)}, s32[1,240]{1,0:T(1,128)}, u32[]{:S(2)}) copy-start(s32[1,240]{1,0:T(1,128)} %param.10) | copy-start | bytes 2884
  2.7 9.6 %collective-permute-start = (bf16[528,512]{1,0:T(8,128)(2,1)}, bf16[528,512]{1,0:T(8,128)(2,1)S(1)}, u32[]{:S(2)}, u32[]{:S(2)}) collective-permute-start(bf16[528,512]{1,0:T(8,128)(2,1)} %get-tuple-element.43), channel_id=1, source_target_pairs={{8,0},{33,1},{10,2},{35,3},{12,4},{37,5},{14,6},{39,7},{16,8},{41,... | collective-permute-start | bytes 1622024 | tf_op jit(solution)/shard_map/ppermute | solution.py:54
  3.3 9.6 %collective-permute-start.2 = (bf16[528,512]{1,0:T(8,128)(2,1)}, bf16[528,512]{1,0:T(8,128)(2,1)S(1)}, u32[]{:S(2)}, u32[]{:S(2)}) collective-permute-start(bf16[528,512]{1,0:T(8,128)(2,1)} %get-tuple-element.44), channel_id=1, source_target_pairs={{24,0},{97,1},{26,2},{99,3},{28,4},{101,5},{30,6},{103,7},{0,8},{1... | collective-permute-start | bytes 1622024 | tf_op jit(solution)/shard_map/ppermute | solution.py:54
  12.3 24.3 %collective-permute-start.1 = (bf16[528,512]{1,0:T(8,128)(2,1)S(1)}, bf16[528,512]{1,0:T(8,128)(2,1)S(1)}, u32[]{:S(2)}, u32[]{:S(2)}) collective-permute-start(bf16[528,512]{1,0:T(8,128)(2,1)S(1)} %collective-permute-done.low1), channel_id=1, source_target_pairs={{8,0},{33,1},{10,2},{35,3},{12,4},{37,5},{14,6},{39,7},{16,8},{41,... | collective-permute-start | bytes 1622024 | tf_op jit(solution)/shard_map/ppermute | solution.py:54
  12.8 23.8 %collective-permute-start.3 = (bf16[528,512]{1,0:T(8,128)(2,1)S(1)}, bf16[528,512]{1,0:T(8,128)(2,1)S(1)}, u32[]{:S(2)}, u32[]{:S(2)}) collective-permute-start(bf16[528,512]{1,0:T(8,128)(2,1)S(1)} %collective-permute-done.2.high3), channel_id=1, source_target_pairs={{24,0},{97,1},{26,2},{99,3},{28,4},{101,5},{30,6},{103,7},{0,8},{1... | collective-permute-start | bytes 1622024 | tf_op jit(solution)/shard_map/ppermute | solution.py:54
  14.7 21.9 %collective-permute-start.8 = (bf16[528,512]{1,0:T(8,128)(2,1)}, bf16[528,512]{1,0:T(8,128)(2,1)}, u32[]{:S(2)}, u32[]{:S(2)}) collective-permute-start(bf16[528,512]{1,0:T(8,128)(2,1)} %get-tuple-element.43), channel_id=1, source_target_pairs={{24,0},{97,1},{26,2},{99,3},{28,4},{101,5},{30,6},{103,7},{0,8},{1... | collective-permute-start | bytes 1622024 | tf_op jit(solution)/shard_map/ppermute | solution.py:54
  18.0 18.7 %collective-permute-start.7 = (bf16[528,512]{1,0:T(8,128)(2,1)}, bf16[528,512]{1,0:T(8,128)(2,1)}, u32[]{:S(2)}, u32[]{:S(2)}) collective-permute-start(bf16[528,512]{1,0:T(8,128)(2,1)} %get-tuple-element.44), channel_id=1, source_target_pairs={{8,0},{33,1},{10,2},{35,3},{12,4},{37,5},{14,6},{39,7},{16,8},{41,... | collective-permute-start | bytes 1622024 | tf_op jit(solution)/shard_map/ppermute | solution.py:54
  22.9 3.6 %collective-permute-start.6 = (s32[16]{0:T(128)S(1)}, s32[16]{0:T(128)S(1)}, u32[]{:S(2)}, u32[]{:S(2)}) collective-permute-start(s32[16]{0:T(128)S(1)} %get-tuple-element.80), channel_id=1, source_target_pairs={{32,0},{9,1},{34,2},{11,3},{36,4},{13,5},{38,6},{15,7},{40,8},{17,... | collective-permute-start | bytes 200 | tf_op jit(solution)/shard_map/ppermute | solution.py:54
  26.5 5.0 %collective-permute-start.5 = (s32[16]{0:T(128)S(1)}, s32[16]{0:T(128)S(1)}, u32[]{:S(2)}, u32[]{:S(2)}) collective-permute-start(s32[16]{0:T(128)S(1)} %get-tuple-element.81), channel_id=1, source_target_pairs={{64,0},{17,1},{66,2},{19,3},{68,4},{21,5},{70,6},{23,7},{72,8},{25... | collective-permute-start | bytes 200 | tf_op jit(solution)/shard_map/ppermute | solution.py:54
  31.6 5.0 %collective-permute-start.4 = (s32[16]{0:T(128)S(1)}, s32[16]{0:T(128)S(1)}, u32[]{:S(2)}, u32[]{:S(2)}) collective-permute-start(s32[16]{0:T(128)S(1)} %get-tuple-element.82), channel_id=1, source_target_pairs={{96,0},{25,1},{98,2},{27,3},{100,4},{29,5},{102,6},{31,7},{104,8},... | collective-permute-start | bytes 200 | tf_op jit(solution)/shard_map/ppermute | solution.py:54
  36.7 7.7 %copy-start.6 = (s32[192,5,128]{2,0,1:T(8,128)S(1)}, s32[192,5,128]{2,0,1:T(8,128)}, u32[]{:S(2)}) copy-start(s32[192,5,128]{2,0,1:T(8,128)} %param.13) | copy-start | bytes 1474564
  38.7 48.3 %collective-permute-start.10 = (bf16[2064,512]{1,0:T(8,128)(2,1)S(1)}, bf16[2064,512]{1,0:T(8,128)(2,1)S(1)}, u32[]{:S(2)}, u32[]{:S(2)}) collective-permute-start(bf16[2064,512]{1,0:T(8,128)(2,1)S(1)} %get-tuple-element.52), channel_id=1, source_target_pairs={{32,0},{9,1},{34,2},{11,3},{36,4},{13,5},{38,6},{15,7},{40,8},{17,... | collective-permute-start | bytes 6340616 | tf_op jit(solution)/shard_map/ppermute | solution.py:54
  40.8 46.2 %collective-permute-start.11 = (bf16[2064,512]{1,0:T(8,128)(2,1)S(1)}, bf16[2064,512]{1,0:T(8,128)(2,1)S(1)}, u32[]{:S(2)}, u32[]{:S(2)}) collective-permute-start(bf16[2064,512]{1,0:T(8,128)(2,1)S(1)} %get-tuple-element.53), channel_id=1, source_target_pairs={{96,0},{25,1},{98,2},{27,3},{100,4},{29,5},{102,6},{31,7},{104,8},... | collective-permute-start | bytes 6340616 | tf_op jit(solution)/shard_map/ppermute | solution.py:54
  40.8 70.5 %collective-permute-start.9 = (bf16[1024,512]{1,0:T(8,128)(2,1)S(1)}, bf16[1024,512]{1,0:T(8,128)(2,1)S(1)}, u32[]{:S(2)}, u32[]{:S(2)}) collective-permute-start(bf16[1024,512]{1,0:T(8,128)(2,1)S(1)} %get-tuple-element.50), channel_id=1, source_target_pairs={{64,0},{17,1},{66,2},{19,3},{68,4},{21,5},{70,6},{23,7},{72,8},{25... | collective-permute-start | bytes 3145736 | tf_op jit(solution)/shard_map/ppermute | solution.py:54
  44.2 70.5 %collective-permute-start.12 = (bf16[1024,512]{1,0:T(8,128)(2,1)S(1)}, bf16[1024,512]{1,0:T(8,128)(2,1)S(1)}, u32[]{:S(2)}, u32[]{:S(2)}) collective-permute-start(bf16[1024,512]{1,0:T(8,128)(2,1)S(1)} %get-tuple-element.57), channel_id=1, source_target_pairs={{64,0},{17,1},{66,2},{19,3},{68,4},{21,5},{70,6},{23,7},{72,8},{25... | collective-permute-start | bytes 3145736 | tf_op jit(solution)/shard_map/ppermute | solution.py:54
  87.1 1.2 collective-permute-start.13
  88.4 3.9 %collective-permute-start.14 = (f32[8,512]{1,0:T(8,128)S(1)}, f32[8,512]{1,0:T(8,128)S(1)}, u32[]{:S(2)}, u32[]{:S(2)}) collective-permute-start(f32[8,512]{1,0:T(8,128)S(1)} %fusion.2), channel_id=1, source_target_pairs={{0,2},{2,0},{4,6},{6,4},{1,3},{3,1},{5,7},{7,5},{8,10},{10,8},{12,... | collective-permute-start | bytes 49160 | tf_op jit(solution)/shard_map/ppermute | solution.py:61
  92.3 5.2 %collective-permute-start.15 = (f32[8,512]{1,0:T(8,128)S(1)}, f32[8,512]{1,0:T(8,128)S(1)}, u32[]{:S(2)}, u32[]{:S(2)}) collective-permute-start(f32[8,512]{1,0:T(8,128)S(1)} %add.35), channel_id=1, source_target_pairs={{0,4},{2,6},{4,0},{6,2},{1,5},{3,7},{5,1},{7,3},{8,12},{10,14},{12... | collective-permute-start | bytes 49160 | tf_op jit(solution)/shard_map/ppermute | solution.py:61
  97.6 17.1 %collective-permute-start.16 = (f32[8,512]{1,0:T(8,128)S(1)}, f32[8,512]{1,0:T(8,128)S(1)}, u32[]{:S(2)}, u32[]{:S(2)}) collective-permute-start(f32[8,512]{1,0:T(8,128)S(1)} %add.36.refs_6_), channel_id=1, source_target_pairs={{80,0},{81,1},{82,2},{83,3},{84,4},{85,5},{86,6},{87,7},{88,8},{89... | collective-permute-start | bytes 49160 | tf_op jit(solution)/shard_map/ppermute | solution.py:54
  111.2 3.5 %copy-start.1 = (f32[1024,512]{1,0:T(8,128)S(1)}, f32[1024,512]{1,0:T(8,128)}, u32[]{:S(2)}) copy-start(f32[1024,512]{1,0:T(8,128)} %refs_5_.1) | copy-start | bytes 6291460
  118.6 9.4 %collective-permute-start.17 = (bf16[528,512]{1,0:T(8,128)(2,1)S(1)}, bf16[528,512]{1,0:T(8,128)(2,1)S(1)}, u32[]{:S(2)}, u32[]{:S(2)}) collective-permute-start(bf16[528,512]{1,0:T(8,128)(2,1)S(1)} %get-tuple-element.61), channel_id=1, source_target_pairs={{8,0},{33,1},{10,2},{35,3},{12,4},{37,5},{14,6},{39,7},{16,8},{41,... | collective-permute-start | bytes 1622024 | tf_op jit(solution)/shard_map/ppermute | solution.py:54
  118.7 9.6 %collective-permute-start.19 = (bf16[528,512]{1,0:T(8,128)(2,1)S(1)}, bf16[528,512]{1,0:T(8,128)(2,1)S(1)}, u32[]{:S(2)}, u32[]{:S(2)}) collective-permute-start(bf16[528,512]{1,0:T(8,128)(2,1)S(1)} %get-tuple-element.62), channel_id=1, source_target_pairs={{24,0},{97,1},{26,2},{99,3},{28,4},{101,5},{30,6},{103,7},{0,8},{1... | collective-permute-start | bytes 1622024 | tf_op jit(solution)/shard_map/ppermute | solution.py:54
  128.0 9.4 %collective-permute-start.18 = (bf16[528,512]{1,0:T(8,128)(2,1)S(1)}, bf16[528,512]{1,0:T(8,128)(2,1)S(1)}, u32[]{:S(2)}, u32[]{:S(2)}) collective-permute-start(bf16[528,512]{1,0:T(8,128)(2,1)S(1)} %collective-permute-done.17.low1), channel_id=1, source_target_pairs={{8,0},{33,1},{10,2},{35,3},{12,4},{37,5},{14,6},{39,7},{16,8},{41,... | collective-permute-start | bytes 1622024 | tf_op jit(solution)/shard_map/ppermute | solution.py:54
  128.3 9.4 %collective-permute-start.20 = (bf16[528,512]{1,0:T(8,128)(2,1)S(1)}, bf16[528,512]{1,0:T(8,128)(2,1)S(1)}, u32[]{:S(2)}, u32[]{:S(2)}) collective-permute-start(bf16[528,512]{1,0:T(8,128)(2,1)S(1)} %collective-permute-done.19.high3), channel_id=1, source_target_pairs={{24,0},{97,1},{26,2},{99,3},{28,4},{101,5},{30,6},{103,7},{0,8},{1... | collective-permute-start | bytes 1622024 | tf_op jit(solution)/shard_map/ppermute | solution.py:54
  130.0 13.4 %collective-permute-start.22 = (bf16[528,512]{1,0:T(8,128)(2,1)S(1)}, bf16[528,512]{1,0:T(8,128)(2,1)S(1)}, u32[]{:S(2)}, u32[]{:S(2)}) collective-permute-start(bf16[528,512]{1,0:T(8,128)(2,1)S(1)} %get-tuple-element.61), channel_id=1, source_target_pairs={{24,0},{97,1},{26,2},{99,3},{28,4},{101,5},{30,6},{103,7},{0,8},{1... | collective-permute-start | bytes 1622024 | tf_op jit(solution)/shard_map/ppermute | solution.py:54
  131.2 12.2 %collective-permute-start.21 = (bf16[528,512]{1,0:T(8,128)(2,1)S(1)}, bf16[528,512]{1,0:T(8,128)(2,1)S(1)}, u32[]{:S(2)}, u32[]{:S(2)}) collective-permute-start(bf16[528,512]{1,0:T(8,128)(2,1)S(1)} %get-tuple-element.62), channel_id=1, source_target_pairs={{8,0},{33,1},{10,2},{35,3},{12,4},{37,5},{14,6},{39,7},{16,8},{41,... | collective-permute-start | bytes 1622024 | tf_op jit(solution)/shard_map/ppermute | solution.py:54
  144.7 26.3 %collective-permute-start.24 = (bf16[2064,512]{1,0:T(8,128)(2,1)S(1)}, bf16[2064,512]{1,0:T(8,128)(2,1)S(1)}, u32[]{:S(2)}, u32[]{:S(2)}) collective-permute-start(bf16[2064,512]{1,0:T(8,128)(2,1)S(1)} %get-tuple-element.69), channel_id=1, source_target_pairs={{32,0},{9,1},{34,2},{11,3},{36,4},{13,5},{38,6},{15,7},{40,8},{17,... | collective-permute-start | bytes 6340616 | tf_op jit(solution)/shard_map/ppermute | solution.py:54
  144.8 50.0 %collective-permute-start.25 = (bf16[2064,512]{1,0:T(8,128)(2,1)S(1)}, bf16[2064,512]{1,0:T(8,128)(2,1)S(1)}, u32[]{:S(2)}, u32[]{:S(2)}) collective-permute-start(bf16[2064,512]{1,0:T(8,128)(2,1)S(1)} %get-tuple-element.70), channel_id=1, source_target_pairs={{96,0},{25,1},{98,2},{27,3},{100,4},{29,5},{102,6},{31,7},{104,8},... | collective-permute-start | bytes 6340616 | tf_op jit(solution)/shard_map/ppermute | solution.py:54
  146.8 70.2 %collective-permute-start.23 = (bf16[1024,512]{1,0:T(8,128)(2,1)S(1)}, bf16[1024,512]{1,0:T(8,128)(2,1)S(1)}, u32[]{:S(2)}, u32[]{:S(2)}) collective-permute-start(bf16[1024,512]{1,0:T(8,128)(2,1)S(1)} %get-tuple-element.67), channel_id=1, source_target_pairs={{64,0},{17,1},{66,2},{19,3},{68,4},{21,5},{70,6},{23,7},{72,8},{25... | collective-permute-start | bytes 3145736 | tf_op jit(solution)/shard_map/ppermute | solution.py:54
  146.8 73.7 %collective-permute-start.26 = (bf16[1024,512]{1,0:T(8,128)(2,1)S(1)}, bf16[1024,512]{1,0:T(8,128)(2,1)S(1)}, u32[]{:S(2)}, u32[]{:S(2)}) collective-permute-start(bf16[1024,512]{1,0:T(8,128)(2,1)S(1)} %get-tuple-element.74), channel_id=1, source_target_pairs={{64,0},{17,1},{66,2},{19,3},{68,4},{21,5},{70,6},{23,7},{72,8},{25... | collective-permute-start | bytes 3145736 | tf_op jit(solution)/shard_map/ppermute | solution.py:54
  194.9 1.2 collective-permute-start.27
  196.2 3.7 %collective-permute-start.28 = (f32[8,512]{1,0:T(8,128)S(1)}, f32[8,512]{1,0:T(8,128)S(1)}, u32[]{:S(2)}, u32[]{:S(2)}) collective-permute-start(f32[8,512]{1,0:T(8,128)S(1)} %fusion.1), channel_id=1, source_target_pairs={{0,2},{2,0},{4,6},{6,4},{1,3},{3,1},{5,7},{7,5},{8,10},{10,8},{12,... | collective-permute-start | bytes 49160 | tf_op jit(solution)/shard_map/ppermute | solution.py:61
  199.9 5.2 %collective-permute-start.29 = (f32[8,512]{1,0:T(8,128)S(1)}, f32[8,512]{1,0:T(8,128)S(1)}, u32[]{:S(2)}, u32[]{:S(2)}) collective-permute-start(f32[8,512]{1,0:T(8,128)S(1)} %add.40), channel_id=1, source_target_pairs={{0,4},{2,6},{4,0},{6,2},{1,5},{3,7},{5,1},{7,3},{8,12},{10,14},{12... | collective-permute-start | bytes 49160 | tf_op jit(solution)/shard_map/ppermute | solution.py:61
  205.2 15.4 %collective-permute-start.30 = (f32[8,512]{1,0:T(8,128)S(1)}, f32[8,512]{1,0:T(8,128)S(1)}, u32[]{:S(2)}, u32[]{:S(2)}) collective-permute-start(f32[8,512]{1,0:T(8,128)S(1)} %add.41.refs_6_), channel_id=1, source_target_pairs={{80,0},{81,1},{82,2},{83,3},{84,4},{85,5},{86,6},{87,7},{88,8},{89... | collective-permute-start | bytes 49160 | tf_op jit(solution)/shard_map/ppermute | solution.py:54
